TPU v7x, 256 devices: a whole 4x4x8 slice. The times are simulated.
256 devices in a mesh: band: 8 (over x, y_lo), space: 32 (over z, y_hi, core).
Axes of the slice: x: 4, y: 4 (y_hi: 2, y_lo: 2; y = y_hi * 2 + y_lo), z: 8, core: 2. Of those that a mesh axis runs over, the one named last changes fastest.
Arguments:
- orbitals: float32 [8, 192, 192, 192], P('band', 'space'), may hold values from -6 to 6
- occupations: int32 [8], replicated, may hold values from 1 to 4
Outputs:
- exchange_potential: float32 [8, 192, 192, 192], P('band', 'space')
All inputs are finite; a program needn't handle non-finite values.
Results may differ from a plain program's by a relative error of at most 0.0003.
Values sent between devices are 32-bit elements; how exact they have to be, the bound alone decides.
No kernel may reach another device: no remote copies, remote signals or barrier semaphores. Data moves between devices by JAX's collectives and lax.ppermute only.
A program may use at most 64 MiB of HBM per device.

v0:
```python
import math

import jax
import jax.numpy as jnp
import ml_dtypes
import numpy as np
from jax import lax
from jax.experimental import pallas as pl
from jax.experimental.pallas import tpu as pltpu
from jax.sharding import PartitionSpec as P

LANES = 128
HALF = 64
SLOTS = 8
VMEM = pl.BlockSpec(memory_space=pltpu.VMEM)
SMEM = pl.BlockSpec(memory_space=pltpu.SMEM)


def tables(length, slabs, rows):
    index = np.arange(length)
    phase = (index[:, None] * index[None, :]) % length * (2.0 * math.pi / length)
    cas = np.cos(phase) + np.sin(phase)
    wide = np.concatenate([np.arange(LANES), np.arange(LANES, length), np.arange(LANES, length)])
    grouped = np.array([rows * slab + row for row in range(rows) for slab in range(slabs)])
    padded = np.zeros((length, slabs, SLOTS))
    padded[:, :, :rows] = cas.reshape(length, slabs, rows)
    padded = padded.reshape(length, slabs * SLOTS)
    parts = {
        "z": cas[:, wide],
        "y": cas[grouped, :],
        "x": padded,
        "xt": padded.T,
        "yt": cas[:, grouped],
        "zt": cas[wide, :],
    }
    places, pieces, start = {}, [], 0
    for name, part in parts.items():
        height, width = part.shape
        places[name] = (start, height, width)
        start += 2 * height
        high = part.astype(ml_dtypes.bfloat16)
        low = (part - high.astype(np.float64)).astype(ml_dtypes.bfloat16)
        both = np.zeros((2 * height, 2 * LANES), ml_dtypes.bfloat16)
        both[:height, :width], both[height:, :width] = high, low
        pieces.append(both)
    return places, jnp.asarray(np.concatenate(pieces))


def terms(table_ref, place):
    start, height, width = place
    return table_ref[start : start + height, :width], table_ref[start + height : start + 2 * height, :width]


def split(value):
    high = value.astype(jnp.bfloat16)
    return high, (value - high.astype(jnp.float32)).astype(jnp.bfloat16)


def product(left, right):
    def dot(a, b):
        return jnp.dot(a, b, preferred_element_type=jnp.float32)

    return dot(left[0], right[0]) + (dot(left[0], right[1]) + dot(left[1], right[0]))


def call(kernel, out_shape, flops, size, in_specs, scratch=()):
    return pl.pallas_call(
        kernel,
        out_shape=out_shape,
        in_specs=in_specs,
        out_specs=jax.tree.map(lambda _: VMEM, out_shape),
        scratch_shapes=list(scratch),
        compiler_params=pltpu.CompilerParams(vmem_limit_bytes=16 * 1024 * 1024),
        cost_estimate=pl.CostEstimate(flops=flops, bytes_accessed=size, transcendentals=0),
    )


def lower_lanes():
    return lax.broadcasted_iota(jnp.int32, (1, LANES), 1) < HALF


def pack(value):
    half = value.shape[0] // 2
    rest = jnp.concatenate([value[:half, LANES:], value[half:, LANES:]], axis=1)
    return jnp.concatenate([value[:, :LANES], rest], axis=0)


def unpack(packed, length):
    rest = packed[length:]
    column = jnp.concatenate([rest[:, :HALF], rest[:, HALF:]], axis=0)
    return jnp.concatenate([packed[:length], column], axis=1)


def packed_shape(rows, length):
    return jax.ShapeDtypeStruct((rows, length * length // LANES, LANES), jnp.float32)


def packed_planes(orbitals):
    rows, length, _ = orbitals.shape

    def kernel(planes, out):
        for plane in range(rows):
            out[plane] = pack(planes[plane])

    return call(kernel, packed_shape(rows, length), 2**18, 2**21, [VMEM])(orbitals)


def forward(own, guests, table):
    places, entries, rows, length = table
    slabs = length // rows
    count = len(guests)
    block = rows * rows * length // LANES
    points = length * length

    def kernel(*refs):
        own_ref, guest_refs, table_ref, out = refs[0], refs[1 : 1 + count], refs[1 + count], refs[-1]
        z_table, y_table = terms(table_ref, places["z"]), terms(table_ref, places["y"])
        lower = lower_lanes()
        corner = (lax.broadcasted_iota(jnp.int32, (slabs, LANES), 0) == 0) & (
            lax.broadcasted_iota(jnp.int32, (slabs, LANES), 1) == 0
        )
        for number, guest in enumerate(guest_refs):
            for plane in range(rows):
                density = own_ref[plane] * guest[plane]
                mean = jnp.sum(density, keepdims=True) * (1.0 / points)
                along = product(split(unpack(density - mean, length)), z_table)
                both = product(y_table, split(along))
                base = number * block + plane
                for row in range(rows):
                    piece = both[slabs * row : slabs * (row + 1), :LANES]
                    if row == 0:
                        piece = piece + jnp.where(corner, mean * float(points), 0.0)
                    out[:, base + rows * row, :] = piece
                for row in range(0, rows, 2):
                    even = both[slabs * row : slabs * (row + 1), LANES:]
                    odd = both[slabs * (row + 1) : slabs * (row + 2), LANES:]
                    out[:, base + rows * (rows + row // 2), :] = jnp.where(lower, even, odd)

    shape = jax.ShapeDtypeStruct((slabs, count * block, LANES), jnp.float32)
    work = call(kernel, shape, count * 12 * length**3 * rows, count * 2**22, [VMEM] * (2 + count))
    return work(own, *guests, entries)


def middle(blocks, pairs, kernel_values, table):
    places, entries, rows, length = table
    slabs = length // rows
    width = kernel_values.shape[1]
    groups = width // LANES
    depth = groups * rows
    tile = 2 * LANES
    lanes = len(pairs) * width

    def kernel(in_ref, values, table_ref, out, lines):
        lines[:, rows:, :] = jnp.zeros((slabs, SLOTS - rows, lanes), jnp.float32)
        for group in range(len(pairs) * groups):
            base = pairs[group // groups] * depth + rows * (group % groups)
            lines[:, :rows, LANES * group : LANES * (group + 1)] = in_ref[:, base : base + rows, :]
        x_table, back_table = terms(table_ref, places["x"]), terms(table_ref, places["xt"])
        for start in range(0, lanes, tile):
            stop = min(start + tile, lanes)
            line = lines[:, :, start:stop].reshape(slabs * SLOTS, stop - start)
            total = jnp.sum(line, axis=0, keepdims=True)
            spectrum = product(x_table, split(line - total * (1.0 / length)))
            first_row = lax.broadcasted_iota(jnp.int32, spectrum.shape, 0) == 0
            spectrum = spectrum + jnp.where(first_row, total, 0.0)
            scaled = [
                spectrum[:, first - start : first - start + LANES] * values[:, first % width : first % width + LANES]
                for first in range(start, stop, LANES)
            ]
            image = jnp.concatenate(scaled, axis=1)
            solved = product(back_table, split(image)).reshape(slabs, SLOTS, stop - start)
            for first in range(start, stop, LANES):
                place = rows * (first // LANES)
                out[:, place : place + rows, :] = solved[:, :rows, first - start : first - start + LANES]

    shape = jax.ShapeDtypeStruct((slabs, len(pairs) * depth, LANES), jnp.float32)
    scratch = [pltpu.VMEM((slabs, SLOTS, lanes), jnp.float32)]
    work = call(kernel, shape, lanes * 12 * length * length, lanes * 2**12, [VMEM] * 3, scratch)
    return work(blocks, kernel_values, entries)


def potential_plane(block_ref, place, rows, y_table, z_table, lower):
    full = jnp.concatenate([block_ref[:, place + rows * row, :] for row in range(rows)], axis=0)
    parts = []
    for row in range(rows // 2):
        shared = block_ref[:, place + rows * (rows + row), :]
        parts.append(jnp.where(lower, shared, 0.0))
        parts.append(jnp.where(lower, 0.0, shared))
    wide = jnp.concatenate([full, jnp.concatenate(parts, axis=0)], axis=1)
    along = product(y_table, split(wide))
    return pack(product(split(along), z_table))


def apply_pairs(blocks, own, guests, weights, table):
    places, entries, rows, length = table
    count = len(guests)
    block = rows * rows * length // LANES

    def kernel(weight, block_ref, own_ref, *refs):
        guest_refs, table_ref, total, sent = refs[:count], refs[count], refs[count + 1], refs[count + 2 :]
        lower = lower_lanes()
        y_table, z_table = terms(table_ref, places["yt"]), terms(table_ref, places["zt"])
        for number in range(count):
            for plane in range(rows):
                field = potential_plane(block_ref, number * block + plane, rows, y_table, z_table, lower)
                term = (weight[number + 1] * guest_refs[number][plane]) * field
                total[plane] = term if number == 0 else total[plane] + term
                sent[number][plane] = (weight[0] * own_ref[plane]) * field

    shape = packed_shape(rows, length)
    work = call(kernel, [shape] * (1 + count), count * 12 * length**3 * rows, count * 2**22, [SMEM] + [VMEM] * (3 + count))
    return work(weights, blocks, own, *guests, entries)


def apply_own(blocks, own, partial, weights, table):
    places, entries, rows, length = table

    def kernel(weight, block_ref, own_ref, part, table_ref, total):
        lower = lower_lanes()
        y_table, z_table = terms(table_ref, places["yt"]), terms(table_ref, places["zt"])
        for plane in range(rows):
            field = potential_plane(block_ref, plane, rows, y_table, z_table, lower)
            total[plane] = part[plane] + (weight[0] * own_ref[plane]) * field

    work = call(kernel, packed_shape(rows, length), 12 * length**3 * rows, 2**22, [SMEM] + [VMEM] * 4)
    return work(weights, blocks, own, partial, entries)


def finish(total, received, rows, length):
    def kernel(total_ref, first, second, out):
        for plane in range(rows):
            out[plane] = -unpack(total_ref[plane] + (first[plane] + second[plane]), length)

    shape = jax.ShapeDtypeStruct((rows, length, length), jnp.float32)
    return call(kernel, shape, 2**20, 2**22, [VMEM] * 3)(total, *received)


def kernel_lines(length, rows, slab):
    width = rows * length
    shape = (length, width)
    column = lax.broadcasted_iota(jnp.int32, shape, 1)
    group, lane = column // LANES, column % LANES
    shared = group >= rows
    row = jnp.where(shared, 2 * (group - rows) + lane // HALF, group)
    third = jnp.where(shared, LANES + lane % HALF, lane)

    def square(index):
        folded = jnp.minimum(index, length - index)
        return folded * folded

    total = square(lax.broadcasted_iota(jnp.int32, shape, 0)) + square(slab * rows + row) + square(third)
    lowest = (2.0 * math.pi / length) ** 2
    values = 1.0 / (lowest * (1.0 + total.astype(jnp.float32)))
    return jnp.where(total > 0, values, jnp.zeros_like(values)) / float(length**3)


def exchange(blocks):
    return lax.all_to_all(blocks, "space", split_axis=0, concat_axis=0, tiled=True)


def shards(orbitals, occupations):
    rows, length = orbitals.shape[1:3]
    slabs = lax.axis_size("space")
    groups = lax.axis_size("band")
    band = lax.axis_index("band")
    table = tables(length, slabs, rows) + (rows, length)

    def shifted(array, by):
        return lax.ppermute(array, "band", [(group, (group + by) % groups) for group in range(groups)])

    own = packed_planes(orbitals[0])
    guests = [shifted(own, -1), shifted(own, 2)]
    picks = jnp.stack([band, (band + 1) % groups, (band + groups - 2) % groups])
    weights = occupations.astype(jnp.float32)[picks]
    kernel_values = kernel_lines(length, rows, lax.axis_index("space"))

    lines = exchange(forward(own, guests + [own], table))
    pair_back = exchange(middle(lines, [0, 1], kernel_values, table))
    own_image = middle(lines, [2], kernel_values, table)
    partial, to_next, to_far = apply_pairs(pair_back, own, guests, weights, table)
    received = [shifted(to_next, 1), shifted(to_far, -2)]
    own_image, partial = lax.optimization_barrier((own_image, partial))
    own_back = exchange(own_image)
    total = apply_own(own_back, own, partial, weights, table)
    return finish(total, received, rows, length)[None]


def solution(mesh):
    placed = (P("band", "space", None, None), P())
    return jax.shard_map(
        shards,
        mesh=mesh,
        in_specs=placed,
        out_specs=P("band", "space", None, None),
        check_vma=False,
    )
```

profile of v0, /device:TPU:1, one launch (start us, length us, event | category | flops | bytes accessed | tf_op | source)
XLA Modules:
  0.0 217.1 jit_solution(12561404892432526383)
XLA Ops:
  0.0 1.4 copy-done.8
  1.4 0.1 shard_map.37.refs_0_.refs_3_.own_ref
  1.5 4.4 %collective-permute-start = (f32[6,288,128]{2,1,0:T(8,128)S(1)}, f32[6,288,128]{2,1,0:T(8,128)S(1)}, u32[]{:S(2)}, u32[]{:S(2)}) collective-permute-start(f32[6,288,128]{2,1,0:T(8,128)S(1)} %shard_map.37.refs_0_.refs_3_.own_ref), channel_id=1, source_target_pairs={{0,224},{32,0},{64,32},{96,64},{128,96},{160,128},{192,160},{224,1... | collective-permute-start | bytes 2654216 | tf_op jit(solution)/shard_map/ppermute | solution.py:269
  5.9 18.3 %collective-permute-done.refs_1_.refs_0_ = f32[6,288,128]{2,1,0:T(8,128)S(1)} collective-permute-done((f32[6,288,128]{2,1,0:T(8,128)S(1)}, f32[6,288,128]{2,1,0:T(8,128)S(1)}, u32[]{:S(2)}, u32[]{:S(2)}) %collective-permute-start) | collective-permute-done | bytes 884768 | tf_op jit(solution)/shard_map/ppermute | solution.py:269
  24.2 3.1 %collective-permute-done.1.refs_2_.refs_1_ = f32[6,288,128]{2,1,0:T(8,128)S(1)} collective-permute-done((f32[6,288,128]{2,1,0:T(8,128)S(1)}, f32[6,288,128]{2,1,0:T(8,128)S(1)}, u32[]{:S(2)}, u32[]{:S(2)}) %collective-permute-start.1) | collective-permute-done | bytes 884768 | tf_op jit(solution)/shard_map/ppermute | solution.py:269
  27.3 4.2 %shard_map.38 = f32[32,162,128]{2,1,0:T(8,128)S(1)} custom-call(f32[6,288,128]{2,1,0:T(8,128)S(1)} %shard_map.37.refs_0_.refs_3_.own_ref, f32[6,288,128]{2,1,0:T(8,128)S(1)} %collective-permute-done.refs_1_.refs_0_, f32[6,288,128]{2,1,0:T(8,128)S(1)} %collective-permute-done.1.refs_2_.refs_1_, f32[6,288,128]{2,1,0:T(8,128)S(1)} %shard_map.37.refs_0_.refs_3_.own_ref, ...), custom_call_target="tpu_custom_call" | custom-call | flops 1528823808 | bytes 12582912 | tf_op jit(solution)/shard_map/pallas_call | solution.py:141
  31.6 1.5 copy-done.1
  33.1 0.9 copy-done.4
  34.0 1.0 copy-done.6
  35.0 12.9 %all-to-all-start = ((f32[32,162,128]{2,1,0:T(8,128)}), f32[32,162,128]{2,1,0:T(8,128)}, u32[]{:S(2)}, u32[]{:S(2)}) async-start(f32[32,162,128]{2,1,0:T(8,128)} %copy-done.1), calls=%async_computation | async-start | bytes 5505024 | tf_op jit(solution)/shard_map/all_to_all | solution.py:258
  47.9 0.3 select_multiply_fusion.values
  48.3 63.3 %all-to-all-done.in_ref = f32[32,162,128]{2,1,0:T(8,128)} async-done(((f32[32,162,128]{2,1,0:T(8,128)}), f32[32,162,128]{2,1,0:T(8,128)}, u32[]{:S(2)}, u32[]{:S(2)}) %all-to-all-start) | async-done | bytes 2654240 | tf_op jit(solution)/shard_map/all_to_all | solution.py:258
  111.6 4.7 %shard_map.40 = f32[32,108,128]{2,1,0:T(8,128)S(1)} custom-call(f32[32,162,128]{2,1,0:T(8,128)} %all-to-all-done.in_ref, f32[192,1152]{1,0:T(8,128)S(1)} %select_multiply_fusion.values, bf16[2560,256]{1,0:T(8,128)(2,1)S(1)} %copy-done), custom_call_target="tpu_custom_call" | custom-call | flops 1019215872 | bytes 9437184 | tf_op jit(solution)/shard_map/pallas_call | solution.py:179
  116.3 1.3 copy-done.2
  117.6 7.0 %all-to-all-start.1 = ((f32[32,108,128]{2,1,0:T(8,128)}), f32[32,108,128]{2,1,0:T(8,128)}, u32[]{:S(2)}, u32[]{:S(2)}) async-start(f32[32,108,128]{2,1,0:T(8,128)} %copy-done.2), calls=%async_computation.1 | async-start | bytes 3670016 | tf_op jit(solution)/shard_map/all_to_all | solution.py:258
  124.7 0.6 gather_fusion
  125.4 3.3 %shard_map.39 = f32[32,54,128]{2,1,0:T(8,128)S(1)} custom-call(f32[32,162,128]{2,1,0:T(8,128)} %all-to-all-done.in_ref, f32[192,1152]{1,0:T(8,128)S(1)} %select_multiply_fusion.values, bf16[2560,256]{1,0:T(8,128)(2,1)S(1)} %copy-done), custom_call_target="tpu_custom_call" | custom-call | flops 509607936 | bytes 4718592 | tf_op jit(solution)/shard_map/pallas_call | solution.py:179
  128.6 0.9 copy-done.3
  129.6 39.6 %all-to-all-done.1.block_ref = f32[32,108,128]{2,1,0:T(8,128)} async-done(((f32[32,108,128]{2,1,0:T(8,128)}), f32[32,108,128]{2,1,0:T(8,128)}, u32[]{:S(2)}, u32[]{:S(2)}) %all-to-all-start.1) | async-done | bytes 1769504 | tf_op jit(solution)/shard_map/all_to_all | solution.py:258
  169.2 1.2 copy-done.5
  170.4 1.2 copy-done.7
  171.5 4.0 %shard_map.41 = (f32[6,288,128]{2,1,0:T(8,128)S(1)}, f32[6,288,128]{2,1,0:T(8,128)S(1)}, f32[6,288,128]{2,1,0:T(8,128)S(1)}) custom-call(f32[3]{0:T(128)S(1)} %gather_fusion, f32[32,108,128]{2,1,0:T(8,128)} %all-to-all-done.1.block_ref, f32[6,288,128]{2,1,0:T(8,128)S(1)} %shard_map.37.refs_0_.refs_3_.own_ref, f32[6,288,128]{2,1,0:T(8,128)S(1)} %copy-done.5, ...), custom_call_target="tpu_custom_call" | custom-call | flops 1019215872 | bytes 8388608 | tf_op jit(solution)/shard_map/pallas_call | solution.py:212
  175.5 1.0 copy-done.9
  176.5 0.9 copy-done.11
  177.4 0.9 copy-done.12
  178.3 6.2 %all-to-all-start.2 = ((f32[32,54,128]{2,1,0:T(8,128)}), f32[32,54,128]{2,1,0:T(8,128)S(1)}, u32[]{:S(2)}, u32[]{:S(2)}) async-start(f32[32,54,128]{2,1,0:T(8,128)} %copy-done.3), calls=%async_computation.2 | async-start | bytes 1835008 | tf_op jit(solution)/shard_map/all_to_all | solution.py:258
  184.6 0.6 collective-permute-start.3
  185.2 24.7 %all-to-all-done.2.block_ref = f32[32,54,128]{2,1,0:T(8,128)S(1)} async-done(((f32[32,54,128]{2,1,0:T(8,128)}), f32[32,54,128]{2,1,0:T(8,128)S(1)}, u32[]{:S(2)}, u32[]{:S(2)}) %all-to-all-start.2) | async-done | bytes 884768 | tf_op jit(solution)/shard_map/all_to_all | solution.py:258
  209.9 1.2 copy-done.10
  211.1 2.0 shard_map.42.total_ref
  213.1 1.4 collective-permute-done.2.first
  214.4 2.6 %shard_map.43 = f32[6,192,192]{2,1,0:T(8,128)} custom-call(f32[6,288,128]{2,1,0:T(8,128)S(1)} %shard_map.42.total_ref, f32[6,288,128]{2,1,0:T(8,128)} %collective-permute-done.2.first, f32[6,288,128]{2,1,0:T(8,128)} %collective-permute-done.3.second), custom_call_target="tpu_custom_call" | custom-call | flops 1048576 | bytes 4194304 | tf_op jit(solution)/shard_map/pallas_call | solution.py:235
  (26 shorter events, 0.2 us)
Async XLA Ops:
  0.0 27.3 %copy-start = (bf16[2560,256]{1,0:T(8,128)(2,1)S(1)}, bf16[2560,256]{1,0:T(8,128)(2,1)}, u32[]{:S(2)}) copy-start(bf16[2560,256]{1,0:T(8,128)(2,1)} %constant.104.clone.refs_4_.table_ref.refs_2_) | copy-start | bytes 3932164
  0.0 1.4 copy-start.8
  1.5 22.7 %collective-permute-start = (f32[6,288,128]{2,1,0:T(8,128)S(1)}, f32[6,288,128]{2,1,0:T(8,128)S(1)}, u32[]{:S(2)}, u32[]{:S(2)}) collective-permute-start(f32[6,288,128]{2,1,0:T(8,128)S(1)} %shard_map.37.refs_0_.refs_3_.own_ref), channel_id=1, source_target_pairs={{0,224},{32,0},{64,32},{96,64},{128,96},{160,128},{192,160},{224,1... | collective-permute-start | bytes 2654216 | tf_op jit(solution)/shard_map/ppermute | solution.py:269
  5.9 21.4 %collective-permute-start.1 = (f32[6,288,128]{2,1,0:T(8,128)S(1)}, f32[6,288,128]{2,1,0:T(8,128)S(1)}, u32[]{:S(2)}, u32[]{:S(2)}) collective-permute-start(f32[6,288,128]{2,1,0:T(8,128)S(1)} %shard_map.37.refs_0_.refs_3_.own_ref), channel_id=1, source_target_pairs={{0,64},{32,96},{64,128},{96,160},{128,192},{160,224},{192,0},{224,... | collective-permute-start | bytes 2654216 | tf_op jit(solution)/shard_map/ppermute | solution.py:269
  31.5 1.6 copy-start.1
  33.1 0.9 copy-start.4
  34.0 1.0 copy-start.6
  35.0 76.6 %all-to-all-start = ((f32[32,162,128]{2,1,0:T(8,128)}), f32[32,162,128]{2,1,0:T(8,128)}, u32[]{:S(2)}, u32[]{:S(2)}) async-start(f32[32,162,128]{2,1,0:T(8,128)} %copy-done.1), calls=%async_computation | async-start | bytes 5505024 | tf_op jit(solution)/shard_map/all_to_all | solution.py:258
  116.3 1.3 copy-start.2
  117.6 7.0 %copy-start.13 = (s32[8]{0:T(128)S(1)}, s32[8]{0:T(128)}, u32[]{:S(2)}) copy-start(s32[8]{0:T(128)} %param.4) | copy-start | bytes 100
  117.6 51.6 %all-to-all-start.1 = ((f32[32,108,128]{2,1,0:T(8,128)}), f32[32,108,128]{2,1,0:T(8,128)}, u32[]{:S(2)}, u32[]{:S(2)}) async-start(f32[32,108,128]{2,1,0:T(8,128)} %copy-done.2), calls=%async_computation.1 | async-start | bytes 3670016 | tf_op jit(solution)/shard_map/all_to_all | solution.py:258
  128.6 0.9 copy-start.3
  169.2 1.2 copy-start.5
  170.4 1.2 copy-start.7
  175.5 1.0 copy-start.9
  176.5 0.9 copy-start.11
  177.4 0.9 copy-start.12
  178.3 31.6 %all-to-all-start.2 = ((f32[32,54,128]{2,1,0:T(8,128)}), f32[32,54,128]{2,1,0:T(8,128)S(1)}, u32[]{:S(2)}, u32[]{:S(2)}) async-start(f32[32,54,128]{2,1,0:T(8,128)} %copy-done.3), calls=%async_computation.2 | async-start | bytes 1835008 | tf_op jit(solution)/shard_map/all_to_all | solution.py:258
  184.5 29.9 %collective-permute-start.2 = (f32[6,288,128]{2,1,0:T(8,128)}, f32[6,288,128]{2,1,0:T(8,128)}, u32[]{:S(2)}, u32[]{:S(2)}) collective-permute-start(f32[6,288,128]{2,1,0:T(8,128)} %copy-done.12), channel_id=1, source_target_pairs={{0,32},{32,64},{64,96},{96,128},{128,160},{160,192},{192,224},{224... | collective-permute-start | bytes 2654216 | tf_op jit(solution)/shard_map/ppermute | solution.py:269
  184.6 29.8 %collective-permute-start.3 = (f32[6,288,128]{2,1,0:T(8,128)}, f32[6,288,128]{2,1,0:T(8,128)}, u32[]{:S(2)}, u32[]{:S(2)}) collective-permute-start(f32[6,288,128]{2,1,0:T(8,128)} %copy-done.11), channel_id=1, source_target_pairs={{0,192},{32,224},{64,0},{96,32},{128,64},{160,96},{192,128},{224,1... | collective-permute-start | bytes 2654216 | tf_op jit(solution)/shard_map/ppermute | solution.py:269
  209.9 1.2 copy-start.10
where the time goes:
time: 220 us; the launch traced here: 217 us
  waiting for transfers between devices  150 us (68%)
  starting transfers between devices  31.1 us (14%)
  Pallas kernels  20.9 us (10%)
  local copies, waits for them, and re-layouts  14 us (6%)
    all_to_all x3, waiting for transfers between devices, exchange(): lax.all_to_all(blocks, 'space', split_axis=0, concat_axis=0, tiled=True)  128 us
    all_to_all x3, starting transfers between devices, exchange(): lax.all_to_all(blocks, 'space', split_axis=0, concat_axis=0, tiled=True)  26 us
    ppermute x4, waiting for transfers between devices, shifted(): lax.ppermute(array, 'band', [(group, (group + by) % groups) for group in...  22.8 us
    unnamed x28, local copies, waits for them, and re-layouts  13.3 us
    pallas_call x2, Pallas kernels, middle(): return work(blocks, kernel_values, entries)  7.97 us
    ppermute x4, starting transfers between devices, shifted(): lax.ppermute(array, 'band', [(group, (group + by) % groups) for group in...  5.05 us
  transfers between devices with their start and end apart: 7, of which 6 were waited for; matrix products, arithmetic and copies ran while one was open for 1% of the time, Pallas kernels for 2%

commit v1 on v0

--- a/solution.py
+++ b/solution.py
@@ -105,7 +105,7 @@
     return call(kernel, packed_shape(rows, length), 2**18, 2**21, [VMEM])(orbitals)
 
 
-def forward(own, guests, table):
+def forward(own, guests, table, weight=1):
     places, entries, rows, length = table
     slabs = length // rows
     count = len(guests)
@@ -137,7 +137,7 @@
                     out[:, base + rows * (rows + row // 2), :] = jnp.where(lower, even, odd)
 
     shape = jax.ShapeDtypeStruct((slabs, count * block, LANES), jnp.float32)
-    work = call(kernel, shape, count * 12 * length**3 * rows, count * 2**22, [VMEM] * (2 + count))
+    work = call(kernel, shape, weight * count * 12 * length**3 * rows, count * 2**22, [VMEM] * (2 + count))
     return work(own, *guests, entries)
 
 
@@ -212,27 +212,30 @@
     return work(weights, blocks, own, *guests, entries)
 
 
-def apply_own(blocks, own, partial, weights, table):
+def add_received(partial, received):
+    rows = partial.shape[0]
+
+    def kernel(part, first, second, out):
+        for plane in range(rows):
+            out[plane] = part[plane] + (first[plane] + second[plane])
+
+    shape = jax.ShapeDtypeStruct(partial.shape, jnp.float32)
+    return call(kernel, shape, 2**34, 2**22, [VMEM] * 3)(partial, *received)
+
+
+def apply_own(blocks, own, others, weights, table):
     places, entries, rows, length = table
 
-    def kernel(weight, block_ref, own_ref, part, table_ref, total):
+    def kernel(weight, block_ref, own_ref, other, table_ref, out):
         lower = lower_lanes()
         y_table, z_table = terms(table_ref, places["yt"]), terms(table_ref, places["zt"])
         for plane in range(rows):
             field = potential_plane(block_ref, plane, rows, y_table, z_table, lower)
-            total[plane] = part[plane] + (weight[0] * own_ref[plane]) * field
-
-    work = call(kernel, packed_shape(rows, length), 12 * length**3 * rows, 2**22, [SMEM] + [VMEM] * 4)
-    return work(weights, blocks, own, partial, entries)
-
-
-def finish(total, received, rows, length):
-    def kernel(total_ref, first, second, out):
-        for plane in range(rows):
-            out[plane] = -unpack(total_ref[plane] + (first[plane] + second[plane]), length)
+            out[plane] = -unpack(other[plane] + (weight[0] * own_ref[plane]) * field, length)
 
     shape = jax.ShapeDtypeStruct((rows, length, length), jnp.float32)
-    return call(kernel, shape, 2**20, 2**22, [VMEM] * 3)(total, *received)
+    work = call(kernel, shape, 12 * length**3 * rows, 2**22, [SMEM] + [VMEM] * 4)
+    return work(weights, blocks, own, others, entries)
 
 
 def kernel_lines(length, rows, slab):
@@ -274,15 +277,18 @@
     weights = occupations.astype(jnp.float32)[picks]
     kernel_values = kernel_lines(length, rows, lax.axis_index("space"))
 
-    lines = exchange(forward(own, guests + [own], table))
-    pair_back = exchange(middle(lines, [0, 1], kernel_values, table))
-    own_image = middle(lines, [2], kernel_values, table)
+    own_lines = exchange(forward(own, [own], table))
+    pair_blocks = forward(own, guests, table, 16)
+    pair_blocks, own_lines = lax.optimization_barrier((pair_blocks, own_lines))
+    pair_lines = exchange(pair_blocks)
+    own_image = middle(own_lines, [0], kernel_values, table)
+    pair_back = exchange(middle(pair_lines, [0, 1], kernel_values, table))
+    own_image, pair_back = lax.optimization_barrier((own_image, pair_back))
+    own_back = exchange(own_image)
     partial, to_next, to_far = apply_pairs(pair_back, own, guests, weights, table)
     received = [shifted(to_next, 1), shifted(to_far, -2)]
-    own_image, partial = lax.optimization_barrier((own_image, partial))
-    own_back = exchange(own_image)
-    total = apply_own(own_back, own, partial, weights, table)
-    return finish(total, received, rows, length)[None]
+    others = add_received(partial, received)
+    return apply_own(own_back, own, others, weights, table)[None]
 
 
 def solution(mesh):

time: 220 us -> 200 us (0.909)
  waiting for transfers between devices: 150 us -> 126 us
  starting transfers between devices: 31.1 us -> 37.5 us
  local copies, waits for them, and re-layouts: 14 us -> 11.6 us
    all_to_all x3 -> x4, waiting for transfers between devices: 128 us -> 101 us  [exchange(): lax.all_to_all(blocks, 'space', split_axis=0, concat_axis=0, tiled=True)]
    all_to_all x3 -> x4, starting transfers between devices: 26 us -> 30.9 us  [exchange(): lax.all_to_all(blocks, 'space', split_axis=0, concat_axis=0, tiled=True)]
    ppermute x4, waiting for transfers between devices: 22.8 us -> 25.1 us  [shifted(): lax.ppermute(array, 'band', [(group, (group + by) % groups) for group in...]
    unnamed x28 -> x24, local copies, waits for them, and re-layouts: 13.3 us -> 11 us
    pallas_call x1 -> x2, Pallas kernels: 4.21 us -> 6.06 us  [forward(): return work(own, *guests, entries)]
  transfers between devices with their start and end apart: 7 -> 8, of which waited for: 6 -> 7; matrix products, arithmetic and copies ran while one was open for 1% -> 1% of each run, Pallas kernels for 2% -> 5%
where the time goes in v1:
time: 200 us; the launch traced here: 199 us
  waiting for transfers between devices  126 us (63%)
  starting transfers between devices  37.5 us (19%)
  Pallas kernels  23 us (12%)
  local copies, waits for them, and re-layouts  11.6 us (6%)
    all_to_all x4, waiting for transfers between devices, exchange(): lax.all_to_all(blocks, 'space', split_axis=0, concat_axis=0, tiled=True)  101 us
    all_to_all x4, starting transfers between devices, exchange(): lax.all_to_all(blocks, 'space', split_axis=0, concat_axis=0, tiled=True)  30.9 us
    ppermute x4, waiting for transfers between devices, shifted(): lax.ppermute(array, 'band', [(group, (group + by) % groups) for group in...  25.1 us
    unnamed x24, local copies, waits for them, and re-layouts  11 us
    pallas_call x2, Pallas kernels, middle(): return work(blocks, kernel_values, entries)  6.83 us
    ppermute x4, starting transfers between devices, shifted(): lax.ppermute(array, 'band', [(group, (group + by) % groups) for group in...  6.58 us
    pallas_call x2, Pallas kernels, forward(): return work(own, *guests, entries)  6.06 us
    pallas_call x1, Pallas kernels, apply_pairs(): return work(weights, blocks, own, *guests, entries)  5.38 us
  transfers between devices with their start and end apart: 8, of which 7 were waited for; matrix products, arithmetic and copies ran while one was open for 1% of the time, Pallas kernels for 5%

profile of v1, /device:TPU:1, one launch (start us, length us, event | category | flops | bytes accessed | tf_op | source)
XLA Modules:
  0.0 198.9 jit_solution(11928178101631260951)
XLA Ops:
  0.0 1.4 copy-done.6
  1.5 2.1 %collective-permute-start.1 = (f32[6,288,128]{2,1,0:T(8,128)S(1)}, f32[6,288,128]{2,1,0:T(8,128)}, u32[]{:S(2)}, u32[]{:S(2)}) collective-permute-start(f32[6,288,128]{2,1,0:T(8,128)S(1)} %shard_map.37.refs_0_.refs_1_.own_ref), channel_id=1, source_target_pairs={{0,64},{32,96},{64,128},{96,160},{128,192},{160,224},{192,0},{224,... | collective-permute-start | bytes 2654216 | tf_op jit(solution)/shard_map/ppermute | solution.py:272
  3.6 2.5 %collective-permute-start = (f32[6,288,128]{2,1,0:T(8,128)S(1)}, f32[6,288,128]{2,1,0:T(8,128)}, u32[]{:S(2)}, u32[]{:S(2)}) collective-permute-start(f32[6,288,128]{2,1,0:T(8,128)S(1)} %shard_map.37.refs_0_.refs_1_.own_ref), channel_id=1, source_target_pairs={{0,224},{32,0},{64,32},{96,64},{128,96},{160,128},{192,160},{224,1... | collective-permute-start | bytes 2654216 | tf_op jit(solution)/shard_map/ppermute | solution.py:272
  6.1 1.7 shard_map.39
  7.9 0.9 copy-done.4
  8.8 12.2 %all-to-all-start = ((f32[32,54,128]{2,1,0:T(8,128)}), f32[32,54,128]{2,1,0:T(8,128)S(1)}, u32[]{:S(2)}, u32[]{:S(2)}) async-start(f32[32,54,128]{2,1,0:T(8,128)} %copy-done.4), calls=%async_computation | async-start | bytes 1835008 | tf_op jit(solution)/shard_map/all_to_all | solution.py:261
  21.0 1.1 collective-permute-done.1.refs_2_.refs_1_
  22.1 2.4 %collective-permute-done.refs_1_.refs_0_ = f32[6,288,128]{2,1,0:T(8,128)} collective-permute-done((f32[6,288,128]{2,1,0:T(8,128)S(1)}, f32[6,288,128]{2,1,0:T(8,128)}, u32[]{:S(2)}, u32[]{:S(2)}) %collective-permute-start) | collective-permute-done | bytes 884768 | tf_op jit(solution)/shard_map/ppermute | solution.py:272
  24.5 4.4 %shard_map.38 = f32[32,108,128]{2,1,0:T(8,128)S(1)} custom-call(f32[6,288,128]{2,1,0:T(8,128)S(1)} %shard_map.37.refs_0_.refs_1_.own_ref, f32[6,288,128]{2,1,0:T(8,128)} %collective-permute-done.refs_1_.refs_0_, f32[6,288,128]{2,1,0:T(8,128)} %collective-permute-done.1.refs_2_.refs_1_, bf16[2560,256]{1,0:T(8,128)(2,1)S(1)} %copy-done), custom_call_target="tpu_custom_call" | custom-call | flops 16307453952 | bytes 8388608 | tf_op jit(solution)/shard_map/pallas_call | solution.py:141
  28.9 1.2 copy-done.5
  30.1 16.2 %all-to-all-done.in_ref = f32[32,54,128]{2,1,0:T(8,128)S(1)} async-done(((f32[32,54,128]{2,1,0:T(8,128)}), f32[32,54,128]{2,1,0:T(8,128)S(1)}, u32[]{:S(2)}, u32[]{:S(2)}) %all-to-all-start) | async-done | bytes 884768 | tf_op jit(solution)/shard_map/all_to_all | solution.py:261
  46.3 0.9 copy-done.2
  47.3 5.9 %all-to-all-start.1 = ((f32[32,108,128]{2,1,0:T(8,128)}), f32[32,108,128]{2,1,0:T(8,128)}, u32[]{:S(2)}, u32[]{:S(2)}) async-start(f32[32,108,128]{2,1,0:T(8,128)} %copy-done.5), calls=%async_computation.1 | async-start | bytes 3670016 | tf_op jit(solution)/shard_map/all_to_all | solution.py:261
  53.3 0.3 select_multiply_fusion.values
  53.6 44.3 %all-to-all-done.1.in_ref = f32[32,108,128]{2,1,0:T(8,128)} async-done(((f32[32,108,128]{2,1,0:T(8,128)}), f32[32,108,128]{2,1,0:T(8,128)}, u32[]{:S(2)}, u32[]{:S(2)}) %all-to-all-start.1) | async-done | bytes 1769504 | tf_op jit(solution)/shard_map/all_to_all | solution.py:261
  97.9 4.4 %shard_map.41 = f32[32,108,128]{2,1,0:T(8,128)S(1)} custom-call(f32[32,108,128]{2,1,0:T(8,128)} %all-to-all-done.1.in_ref, f32[192,1152]{1,0:T(8,128)S(1)} %select_multiply_fusion.values, bf16[2560,256]{1,0:T(8,128)(2,1)S(1)} %copy-done), custom_call_target="tpu_custom_call" | custom-call | flops 1019215872 | bytes 9437184 | tf_op jit(solution)/shard_map/pallas_call | solution.py:179
  102.3 1.2 copy-done.1
  103.5 6.3 %all-to-all-start.2 = ((f32[32,108,128]{2,1,0:T(8,128)}), f32[32,108,128]{2,1,0:T(8,128)}, u32[]{:S(2)}, u32[]{:S(2)}) async-start(f32[32,108,128]{2,1,0:T(8,128)} %copy-done.1), calls=%async_computation.2 | async-start | bytes 3670016 | tf_op jit(solution)/shard_map/all_to_all | solution.py:261
  110.0 0.6 gather_fusion
  110.7 1.2 copy-done.3
  111.8 2.4 %shard_map.40 = f32[32,54,128]{2,1,0:T(8,128)} custom-call(f32[32,54,128]{2,1,0:T(8,128)S(1)} %copy-done.3, f32[192,1152]{1,0:T(8,128)S(1)} %select_multiply_fusion.values, bf16[2560,256]{1,0:T(8,128)(2,1)S(1)} %copy-done), custom_call_target="tpu_custom_call" | custom-call | flops 509607936 | bytes 4718592 | tf_op jit(solution)/shard_map/pallas_call | solution.py:179
  114.2 40.3 %all-to-all-done.2.block_ref = f32[32,108,128]{2,1,0:T(8,128)} async-done(((f32[32,108,128]{2,1,0:T(8,128)}), f32[32,108,128]{2,1,0:T(8,128)}, u32[]{:S(2)}, u32[]{:S(2)}) %all-to-all-start.2) | async-done | bytes 1769504 | tf_op jit(solution)/shard_map/all_to_all | solution.py:261
  154.5 5.4 %shard_map.42 = (f32[6,288,128]{2,1,0:T(8,128)S(1)}, f32[6,288,128]{2,1,0:T(8,128)}, f32[6,288,128]{2,1,0:T(8,128)}) custom-call(f32[3]{0:T(128)S(1)} %gather_fusion, f32[32,108,128]{2,1,0:T(8,128)} %all-to-all-done.2.block_ref, f32[6,288,128]{2,1,0:T(8,128)S(1)} %shard_map.37.refs_0_.refs_1_.own_ref, f32[6,288,128]{2,1,0:T(8,128)} %collective-permute-done.refs_1_.refs_0_, ...), custom_call_target="tpu_custom_call" | custom-call | flops 1019215872 | bytes 8388608 | tf_op jit(solution)/shard_map/pallas_call | solution.py:212
  159.9 0.9 copy-done.9
  160.8 2.0 collective-permute-start.3
  162.8 6.5 %all-to-all-start.3 = ((f32[32,54,128]{2,1,0:T(8,128)}), f32[32,54,128]{2,1,0:T(8,128)S(1)}, u32[]{:S(2)}, u32[]{:S(2)}) async-start(f32[32,54,128]{2,1,0:T(8,128)} %shard_map.40), calls=%async_computation.3 | async-start | bytes 1835008 | tf_op jit(solution)/shard_map/all_to_all | solution.py:261
  169.3 21.5 %collective-permute-done.2.first = f32[6,288,128]{2,1,0:T(8,128)} collective-permute-done((f32[6,288,128]{2,1,0:T(8,128)}, f32[6,288,128]{2,1,0:T(8,128)}, u32[]{:S(2)}, u32[]{:S(2)}) %collective-permute-start.2) | collective-permute-done | bytes 884768 | tf_op jit(solution)/shard_map/ppermute | solution.py:272
  190.8 1.2 copy-done.10
  192.0 1.6 shard_map.43.other
  193.6 0.9 copy-done.7
  194.7 1.2 copy-done.8
  195.8 3.1 %shard_map.44 = f32[6,192,192]{2,1,0:T(8,128)} custom-call(f32[3]{0:T(128)S(1)} %gather_fusion, f32[32,54,128]{2,1,0:T(8,128)S(1)} %all-to-all-done.3.block_ref, f32[6,288,128]{2,1,0:T(8,128)S(1)} %shard_map.37.refs_0_.refs_1_.own_ref, f32[6,288,128]{2,1,0:T(8,128)S(1)} %copy-done.8, bf16[2560,256]{1,0:T(8,128)(2,1)S(1)} %copy-done), custom_call_target="tpu_custom_call" | custom-call | flops 509607936 | bytes 4194304 | tf_op jit(solution)/shard_map/pallas_call | solution.py:238
  (25 shorter events, 0.5 us)
Async XLA Ops:
  0.0 6.1 %copy-start = (bf16[2560,256]{1,0:T(8,128)(2,1)S(1)}, bf16[2560,256]{1,0:T(8,128)(2,1)}, u32[]{:S(2)}) copy-start(bf16[2560,256]{1,0:T(8,128)(2,1)} %constant.104.clone.refs_3_.refs_2_.table_ref) | copy-start | bytes 3932164
  0.0 1.4 copy-start.6
  1.5 20.6 %collective-permute-start.1 = (f32[6,288,128]{2,1,0:T(8,128)S(1)}, f32[6,288,128]{2,1,0:T(8,128)}, u32[]{:S(2)}, u32[]{:S(2)}) collective-permute-start(f32[6,288,128]{2,1,0:T(8,128)S(1)} %shard_map.37.refs_0_.refs_1_.own_ref), channel_id=1, source_target_pairs={{0,64},{32,96},{64,128},{96,160},{128,192},{160,224},{192,0},{224,... | collective-permute-start | bytes 2654216 | tf_op jit(solution)/shard_map/ppermute | solution.py:272
  3.6 20.9 %collective-permute-start = (f32[6,288,128]{2,1,0:T(8,128)S(1)}, f32[6,288,128]{2,1,0:T(8,128)}, u32[]{:S(2)}, u32[]{:S(2)}) collective-permute-start(f32[6,288,128]{2,1,0:T(8,128)S(1)} %shard_map.37.refs_0_.refs_1_.own_ref), channel_id=1, source_target_pairs={{0,224},{32,0},{64,32},{96,64},{128,96},{160,128},{192,160},{224,1... | collective-permute-start | bytes 2654216 | tf_op jit(solution)/shard_map/ppermute | solution.py:272
  7.8 0.9 copy-start.4
  8.8 37.6 %all-to-all-start = ((f32[32,54,128]{2,1,0:T(8,128)}), f32[32,54,128]{2,1,0:T(8,128)S(1)}, u32[]{:S(2)}, u32[]{:S(2)}) async-start(f32[32,54,128]{2,1,0:T(8,128)} %copy-done.4), calls=%async_computation | async-start | bytes 1835008 | tf_op jit(solution)/shard_map/all_to_all | solution.py:261
  28.9 1.2 copy-start.5
  46.3 0.9 copy-start.2
  47.3 50.6 %all-to-all-start.1 = ((f32[32,108,128]{2,1,0:T(8,128)}), f32[32,108,128]{2,1,0:T(8,128)}, u32[]{:S(2)}, u32[]{:S(2)}) async-start(f32[32,108,128]{2,1,0:T(8,128)} %copy-done.5), calls=%async_computation.1 | async-start | bytes 3670016 | tf_op jit(solution)/shard_map/all_to_all | solution.py:261
  102.3 1.2 copy-start.1
  103.5 6.4 %copy-start.11 = (s32[8]{0:T(128)S(1)}, s32[8]{0:T(128)}, u32[]{:S(2)}) copy-start(s32[8]{0:T(128)} %param.4) | copy-start | bytes 100
  103.5 51.0 %all-to-all-start.2 = ((f32[32,108,128]{2,1,0:T(8,128)}), f32[32,108,128]{2,1,0:T(8,128)}, u32[]{:S(2)}, u32[]{:S(2)}) async-start(f32[32,108,128]{2,1,0:T(8,128)} %copy-done.1), calls=%async_computation.2 | async-start | bytes 3670016 | tf_op jit(solution)/shard_map/all_to_all | solution.py:261
  110.7 1.2 copy-start.3
  159.9 0.9 copy-start.9
  160.8 30.0 %collective-permute-start.2 = (f32[6,288,128]{2,1,0:T(8,128)}, f32[6,288,128]{2,1,0:T(8,128)}, u32[]{:S(2)}, u32[]{:S(2)}) collective-permute-start(f32[6,288,128]{2,1,0:T(8,128)} %get-tuple-element.17), channel_id=1, source_target_pairs={{0,32},{32,64},{64,96},{96,128},{128,160},{160,192},{192,224},{224... | collective-permute-start | bytes 2654216 | tf_op jit(solution)/shard_map/ppermute | solution.py:272
  160.8 30.0 %collective-permute-start.3 = (f32[6,288,128]{2,1,0:T(8,128)}, f32[6,288,128]{2,1,0:T(8,128)}, u32[]{:S(2)}, u32[]{:S(2)}) collective-permute-start(f32[6,288,128]{2,1,0:T(8,128)} %get-tuple-element.18), channel_id=1, source_target_pairs={{0,192},{32,224},{64,0},{96,32},{128,64},{160,96},{192,128},{224,1... | collective-permute-start | bytes 2654216 | tf_op jit(solution)/shard_map/ppermute | solution.py:272
  162.8 31.9 %all-to-all-start.3 = ((f32[32,54,128]{2,1,0:T(8,128)}), f32[32,54,128]{2,1,0:T(8,128)S(1)}, u32[]{:S(2)}, u32[]{:S(2)}) async-start(f32[32,54,128]{2,1,0:T(8,128)} %shard_map.40), calls=%async_computation.3 | async-start | bytes 1835008 | tf_op jit(solution)/shard_map/all_to_all | solution.py:261
  190.8 1.2 copy-start.10
  193.6 0.9 copy-start.7
  194.7 1.2 copy-start.8

commit v2 on v1

--- a/solution.py
+++ b/solution.py
@@ -105,11 +105,16 @@
     return call(kernel, packed_shape(rows, length), 2**18, 2**21, [VMEM])(orbitals)
 
 
+def block_pitch(depth):
+    return depth
+
+
 def forward(own, guests, table, weight=1):
     places, entries, rows, length = table
     slabs = length // rows
     count = len(guests)
     block = rows * rows * length // LANES
+    pitch = block_pitch(count * block)
     points = length * length
 
     def kernel(*refs):
@@ -130,13 +135,14 @@
                     piece = both[slabs * row : slabs * (row + 1), :LANES]
                     if row == 0:
                         piece = piece + jnp.where(corner, mean * float(points), 0.0)
-                    out[:, base + rows * row, :] = piece
+                    out[pl.ds(base + rows * row, slabs, stride=pitch), :] = piece
                 for row in range(0, rows, 2):
                     even = both[slabs * row : slabs * (row + 1), LANES:]
                     odd = both[slabs * (row + 1) : slabs * (row + 2), LANES:]
-                    out[:, base + rows * (rows + row // 2), :] = jnp.where(lower, even, odd)
-
-    shape = jax.ShapeDtypeStruct((slabs, count * block, LANES), jnp.float32)
+                    place = base + rows * (rows + row // 2)
+                    out[pl.ds(place, slabs, stride=pitch), :] = jnp.where(lower, even, odd)
+
+    shape = jax.ShapeDtypeStruct((slabs * pitch, LANES), jnp.float32)
     work = call(kernel, shape, weight * count * 12 * length**3 * rows, count * 2**22, [VMEM] * (2 + count))
     return work(own, *guests, entries)
 
@@ -150,14 +156,19 @@
     tile = 2 * LANES
     lanes = len(pairs) * width
 
+    pitch_in, pitch_out = blocks.shape[0] // slabs, block_pitch(len(pairs) * depth)
+
     def kernel(in_ref, values, table_ref, out, lines):
         lines[:, rows:, :] = jnp.zeros((slabs, SLOTS - rows, lanes), jnp.float32)
-        for group in range(len(pairs) * groups):
-            base = pairs[group // groups] * depth + rows * (group % groups)
-            lines[:, :rows, LANES * group : LANES * (group + 1)] = in_ref[:, base : base + rows, :]
         x_table, back_table = terms(table_ref, places["x"]), terms(table_ref, places["xt"])
         for start in range(0, lanes, tile):
             stop = min(start + tile, lanes)
+            for first in range(start, stop, LANES):
+                group = first // LANES
+                base = pairs[group // groups] * depth + rows * (group % groups)
+                for slab in range(slabs):
+                    place = slab * pitch_in + base
+                    lines[slab, :rows, first : first + LANES] = in_ref[place : place + rows, :]
             line = lines[:, :, start:stop].reshape(slabs * SLOTS, stop - start)
             total = jnp.sum(line, axis=0, keepdims=True)
             spectrum = product(x_table, split(line - total * (1.0 / length)))
@@ -170,20 +181,26 @@
             image = jnp.concatenate(scaled, axis=1)
             solved = product(back_table, split(image)).reshape(slabs, SLOTS, stop - start)
             for first in range(start, stop, LANES):
-                place = rows * (first // LANES)
-                out[:, place : place + rows, :] = solved[:, :rows, first - start : first - start + LANES]
-
-    shape = jax.ShapeDtypeStruct((slabs, len(pairs) * depth, LANES), jnp.float32)
+                for slab in range(slabs):
+                    place = slab * pitch_out + rows * (first // LANES)
+                    out[place : place + rows, :] = solved[slab, :rows, first - start : first - start + LANES]
+
+    shape = jax.ShapeDtypeStruct((slabs * pitch_out, LANES), jnp.float32)
     scratch = [pltpu.VMEM((slabs, SLOTS, lanes), jnp.float32)]
     work = call(kernel, shape, lanes * 12 * length * length, lanes * 2**12, [VMEM] * 3, scratch)
     return work(blocks, kernel_values, entries)
 
 
-def potential_plane(block_ref, place, rows, y_table, z_table, lower):
-    full = jnp.concatenate([block_ref[:, place + rows * row, :] for row in range(rows)], axis=0)
+def potential_plane(block_ref, place, rows, slabs, y_table, z_table, lower):
+    pitch = block_ref.shape[0] // slabs
+
+    def across(row):
+        return block_ref[pl.ds(place + rows * row, slabs, stride=pitch), :]
+
+    full = jnp.concatenate([across(row) for row in range(rows)], axis=0)
     parts = []
     for row in range(rows // 2):
-        shared = block_ref[:, place + rows * (rows + row), :]
+        shared = across(rows + row)
         parts.append(jnp.where(lower, shared, 0.0))
         parts.append(jnp.where(lower, 0.0, shared))
     wide = jnp.concatenate([full, jnp.concatenate(parts, axis=0)], axis=1)
@@ -202,7 +219,7 @@
         y_table, z_table = terms(table_ref, places["yt"]), terms(table_ref, places["zt"])
         for number in range(count):
             for plane in range(rows):
-                field = potential_plane(block_ref, number * block + plane, rows, y_table, z_table, lower)
+                field = potential_plane(block_ref, number * block + plane, rows, length // rows, y_table, z_table, lower)
                 term = (weight[number + 1] * guest_refs[number][plane]) * field
                 total[plane] = term if number == 0 else total[plane] + term
                 sent[number][plane] = (weight[0] * own_ref[plane]) * field
@@ -230,7 +247,7 @@
         lower = lower_lanes()
         y_table, z_table = terms(table_ref, places["yt"]), terms(table_ref, places["zt"])
         for plane in range(rows):
-            field = potential_plane(block_ref, plane, rows, y_table, z_table, lower)
+            field = potential_plane(block_ref, plane, rows, length // rows, y_table, z_table, lower)
             out[plane] = -unpack(other[plane] + (weight[0] * own_ref[plane]) * field, length)
 
     shape = jax.ShapeDtypeStruct((rows, length, length), jnp.float32)
@@ -258,7 +275,11 @@
 
 
 def exchange(blocks):
-    return lax.all_to_all(blocks, "space", split_axis=0, concat_axis=0, tiled=True)
+    slabs = lax.axis_size("space")
+    count = blocks.shape[0] // slabs
+    group = math.gcd(count, SLOTS)
+    cut = blocks.reshape(slabs, count // group, group, LANES)
+    return lax.all_to_all(cut, "space", split_axis=0, concat_axis=0, tiled=True).reshape(blocks.shape)
 
 
 def shards(orbitals, occupations):
@@ -282,6 +303,7 @@
     pair_blocks, own_lines = lax.optimization_barrier((pair_blocks, own_lines))
     pair_lines = exchange(pair_blocks)
     own_image = middle(own_lines, [0], kernel_values, table)
+    pair_lines, own_image = lax.optimization_barrier((pair_lines, own_image))
     pair_back = exchange(middle(pair_lines, [0, 1], kernel_values, table))
     own_image, pair_back = lax.optimization_barrier((own_image, pair_back))
     own_back = exchange(own_image)

time: 200 us -> 196 us (0.980)
  waiting for transfers between devices: 126 us -> 122 us
    all_to_all x4, waiting for transfers between devices: 101 us -> 95 us  [exchange(): lax.all_to_all(cut, 'space', split_axis=0, concat_axis=0, tiled=True)]
    ppermute x4, waiting for transfers between devices: 25.1 us -> 27.4 us  [shifted(): lax.ppermute(array, 'band', [(group, (group + by) % groups) for group in...]
where the time goes in v2:
time: 196 us; the launch traced here: 195 us
  waiting for transfers between devices  122 us (62%)
  starting transfers between devices  38.5 us (20%)
  Pallas kernels  22.2 us (11%)
  local copies, waits for them, and re-layouts  11.6 us (6%)
    all_to_all x4, waiting for transfers between devices, exchange(): lax.all_to_all(cut, 'space', split_axis=0, concat_axis=0, tiled=True)  95 us
    all_to_all x4, starting transfers between devices, exchange(): lax.all_to_all(cut, 'space', split_axis=0, concat_axis=0, tiled=True)  30.4 us
    ppermute x4, waiting for transfers between devices, shifted(): lax.ppermute(array, 'band', [(group, (group + by) % groups) for group in...  27.4 us
    unnamed x24, local copies, waits for them, and re-layouts  11 us
    ppermute x4, starting transfers between devices, shifted(): lax.ppermute(array, 'band', [(group, (group + by) % groups) for group in...  8.05 us
    pallas_call x2, Pallas kernels, middle(): return work(blocks, kernel_values, entries)  6.79 us
    pallas_call x2, Pallas kernels, forward(): return work(own, *guests, entries)  5.47 us
    pallas_call x1, Pallas kernels, apply_pairs(): return work(weights, blocks, own, *guests, entries)  5.22 us
  transfers between devices with their start and end apart: 8, of which 7 were waited for; matrix products, arithmetic and copies ran while one was open for 1% of the time, Pallas kernels for 5%

profile of v2, /device:TPU:1, one launch (start us, length us, event | category | flops | bytes accessed | tf_op | source)
XLA Modules:
  0.0 195.3 jit_solution(17643008445239987530)
XLA Ops:
  0.0 1.4 copy-done.6
  1.5 4.4 %collective-permute-start = (f32[6,288,128]{2,1,0:T(8,128)S(1)}, f32[6,288,128]{2,1,0:T(8,128)}, u32[]{:S(2)}, u32[]{:S(2)}) collective-permute-start(f32[6,288,128]{2,1,0:T(8,128)S(1)} %shard_map.37.refs_0_.refs_1_.own_ref), channel_id=1, source_target_pairs={{0,224},{32,0},{64,32},{96,64},{128,96},{160,128},{192,160},{224,1... | collective-permute-start | bytes 2654216 | tf_op jit(solution)/shard_map/ppermute | solution.py:293
  5.9 1.5 shard_map.39
  7.5 0.9 copy-done.4
  8.4 11.9 %all-to-all-start = ((f32[32,27,2,128]{3,2,1,0:T(2,128)}), f32[32,27,2,128]{3,2,1,0:T(2,128)S(1)}, u32[]{:S(2)}, u32[]{:S(2)}) async-start(f32[32,27,2,128]{3,2,1,0:T(2,128)} %bitcast.17), calls=%async_computation | async-start | bytes 1769472 | tf_op jit(solution)/shard_map/all_to_all | solution.py:282
  20.3 3.9 %collective-permute-done.refs_1_.refs_0_ = f32[6,288,128]{2,1,0:T(8,128)} collective-permute-done((f32[6,288,128]{2,1,0:T(8,128)S(1)}, f32[6,288,128]{2,1,0:T(8,128)}, u32[]{:S(2)}, u32[]{:S(2)}) %collective-permute-start) | collective-permute-done | bytes 884768 | tf_op jit(solution)/shard_map/ppermute | solution.py:293
  24.2 3.2 %collective-permute-done.1.refs_2_.refs_1_ = f32[6,288,128]{2,1,0:T(8,128)} collective-permute-done((f32[6,288,128]{2,1,0:T(8,128)S(1)}, f32[6,288,128]{2,1,0:T(8,128)}, u32[]{:S(2)}, u32[]{:S(2)}) %collective-permute-start.1) | collective-permute-done | bytes 884768 | tf_op jit(solution)/shard_map/ppermute | solution.py:293
  27.4 3.9 %shard_map.38 = f32[3456,128]{1,0:T(8,128)S(1)} custom-call(f32[6,288,128]{2,1,0:T(8,128)S(1)} %shard_map.37.refs_0_.refs_1_.own_ref, f32[6,288,128]{2,1,0:T(8,128)} %collective-permute-done.refs_1_.refs_0_, f32[6,288,128]{2,1,0:T(8,128)} %collective-permute-done.1.refs_2_.refs_1_, bf16[2560,256]{1,0:T(8,128)(2,1)S(1)} %copy-done), custom_call_target="tpu_custom_call" | custom-call | flops 16307453952 | bytes 8388608 | tf_op jit(solution)/shard_map/pallas_call | solution.py:147
  31.4 1.2 copy-done.5
  32.6 12.4 %all-to-all-done = f32[32,27,2,128]{3,2,1,0:T(2,128)S(1)} async-done(((f32[32,27,2,128]{3,2,1,0:T(2,128)}), f32[32,27,2,128]{3,2,1,0:T(2,128)S(1)}, u32[]{:S(2)}, u32[]{:S(2)}) %all-to-all-start) | async-done | bytes 884768 | tf_op jit(solution)/shard_map/all_to_all | solution.py:282
  45.0 0.9 copy-done.2
  45.9 5.8 %all-to-all-start.1 = ((f32[32,27,4,128]{3,2,1,0:T(4,128)}), f32[32,27,4,128]{3,2,1,0:T(4,128)}, u32[]{:S(2)}, u32[]{:S(2)}) async-start(f32[32,27,4,128]{3,2,1,0:T(4,128)} %bitcast.19), calls=%async_computation.1 | async-start | bytes 3538944 | tf_op jit(solution)/shard_map/all_to_all | solution.py:282
  51.7 0.3 select_multiply_fusion.values
  52.1 1.2 copy-done.3
  53.2 2.4 %shard_map.40 = f32[1728,128]{1,0:T(8,128)} custom-call(f32[1728,128]{1,0:T(8,128)S(1)} %bitcast.16, f32[192,1152]{1,0:T(8,128)S(1)} %select_multiply_fusion.values, bf16[2560,256]{1,0:T(8,128)(2,1)S(1)} %copy-done), custom_call_target="tpu_custom_call" | custom-call | flops 509607936 | bytes 4718592 | tf_op jit(solution)/shard_map/pallas_call | solution.py:191
  55.6 39.4 %all-to-all-done.1 = f32[32,27,4,128]{3,2,1,0:T(4,128)} async-done(((f32[32,27,4,128]{3,2,1,0:T(4,128)}), f32[32,27,4,128]{3,2,1,0:T(4,128)}, u32[]{:S(2)}, u32[]{:S(2)}) %all-to-all-start.1) | async-done | bytes 1769504 | tf_op jit(solution)/shard_map/all_to_all | solution.py:282
  95.0 4.4 %shard_map.41 = f32[3456,128]{1,0:T(8,128)S(1)} custom-call(f32[3456,128]{1,0:T(8,128)} %bitcast.8.in_ref, f32[192,1152]{1,0:T(8,128)S(1)} %select_multiply_fusion.values, bf16[2560,256]{1,0:T(8,128)(2,1)S(1)} %copy-done), custom_call_target="tpu_custom_call" | custom-call | flops 1019215872 | bytes 9437184 | tf_op jit(solution)/shard_map/pallas_call | solution.py:191
  99.4 1.2 copy-done.1
  100.6 6.3 %all-to-all-start.2 = ((f32[32,27,4,128]{3,2,1,0:T(4,128)}), f32[32,27,4,128]{3,2,1,0:T(4,128)}, u32[]{:S(2)}, u32[]{:S(2)}) async-start(f32[32,27,4,128]{3,2,1,0:T(4,128)} %bitcast.15), calls=%async_computation.2 | async-start | bytes 3538944 | tf_op jit(solution)/shard_map/all_to_all | solution.py:282
  107.1 0.6 gather_fusion
  107.7 42.5 %all-to-all-done.2 = f32[32,27,4,128]{3,2,1,0:T(4,128)} async-done(((f32[32,27,4,128]{3,2,1,0:T(4,128)}), f32[32,27,4,128]{3,2,1,0:T(4,128)}, u32[]{:S(2)}, u32[]{:S(2)}) %all-to-all-start.2) | async-done | bytes 1769504 | tf_op jit(solution)/shard_map/all_to_all | solution.py:282
  150.2 5.2 %shard_map.42 = (f32[6,288,128]{2,1,0:T(8,128)S(1)}, f32[6,288,128]{2,1,0:T(8,128)}, f32[6,288,128]{2,1,0:T(8,128)}) custom-call(f32[3]{0:T(128)S(1)} %gather_fusion, f32[3456,128]{1,0:T(8,128)} %bitcast.10.block_ref, f32[6,288,128]{2,1,0:T(8,128)S(1)} %shard_map.37.refs_0_.refs_1_.own_ref, f32[6,288,128]{2,1,0:T(8,128)} %collective-permute-done.refs_1_.refs_0_, ...), custom_call_target="tpu_custom_call" | custom-call | flops 1019215872 | bytes 8388608 | tf_op jit(solution)/shard_map/pallas_call | solution.py:229
  155.4 0.9 copy-done.9
  156.3 3.7 %collective-permute-start.3 = (f32[6,288,128]{2,1,0:T(8,128)}, f32[6,288,128]{2,1,0:T(8,128)}, u32[]{:S(2)}, u32[]{:S(2)}) collective-permute-start(f32[6,288,128]{2,1,0:T(8,128)} %get-tuple-element.22), channel_id=1, source_target_pairs={{0,192},{32,224},{64,0},{96,32},{128,64},{160,96},{192,128},{224,1... | collective-permute-start | bytes 2654216 | tf_op jit(solution)/shard_map/ppermute | solution.py:293
  160.0 6.4 %all-to-all-start.3 = ((f32[32,27,2,128]{3,2,1,0:T(2,128)}), f32[32,27,2,128]{3,2,1,0:T(2,128)S(1)}, u32[]{:S(2)}, u32[]{:S(2)}) async-start(f32[32,27,2,128]{3,2,1,0:T(2,128)} %bitcast.11), calls=%async_computation.3 | async-start | bytes 1769472 | tf_op jit(solution)/shard_map/all_to_all | solution.py:282
  166.4 20.2 %collective-permute-done.2.first = f32[6,288,128]{2,1,0:T(8,128)} collective-permute-done((f32[6,288,128]{2,1,0:T(8,128)}, f32[6,288,128]{2,1,0:T(8,128)}, u32[]{:S(2)}, u32[]{:S(2)}) %collective-permute-start.2) | collective-permute-done | bytes 884768 | tf_op jit(solution)/shard_map/ppermute | solution.py:293
  186.7 1.2 copy-done.10
  187.8 1.6 shard_map.43.other
  189.4 0.9 copy-done.7
  190.3 0.8 all-to-all-done.3
  191.1 1.2 copy-done.8
  192.3 3.0 %shard_map.44 = f32[6,192,192]{2,1,0:T(8,128)} custom-call(f32[3]{0:T(128)S(1)} %gather_fusion, f32[1728,128]{1,0:T(8,128)S(1)} %bitcast.18, f32[6,288,128]{2,1,0:T(8,128)S(1)} %shard_map.37.refs_0_.refs_1_.own_ref, f32[6,288,128]{2,1,0:T(8,128)S(1)} %copy-done.8, bf16[2560,256]{1,0:T(8,128)(2,1)S(1)} %copy-done), custom_call_target="tpu_custom_call" | custom-call | flops 509607936 | bytes 4194304 | tf_op jit(solution)/shard_map/pallas_call | solution.py:255
  (25 shorter events, 0.3 us)
Async XLA Ops:
  0.0 5.9 %copy-start = (bf16[2560,256]{1,0:T(8,128)(2,1)S(1)}, bf16[2560,256]{1,0:T(8,128)(2,1)}, u32[]{:S(2)}) copy-start(bf16[2560,256]{1,0:T(8,128)(2,1)} %constant.104.clone.refs_3_.refs_2_.table_ref) | copy-start | bytes 3932164
  0.0 1.4 copy-start.6
  1.5 22.7 %collective-permute-start = (f32[6,288,128]{2,1,0:T(8,128)S(1)}, f32[6,288,128]{2,1,0:T(8,128)}, u32[]{:S(2)}, u32[]{:S(2)}) collective-permute-start(f32[6,288,128]{2,1,0:T(8,128)S(1)} %shard_map.37.refs_0_.refs_1_.own_ref), channel_id=1, source_target_pairs={{0,224},{32,0},{64,32},{96,64},{128,96},{160,128},{192,160},{224,1... | collective-permute-start | bytes 2654216 | tf_op jit(solution)/shard_map/ppermute | solution.py:293
  5.9 21.5 %collective-permute-start.1 = (f32[6,288,128]{2,1,0:T(8,128)S(1)}, f32[6,288,128]{2,1,0:T(8,128)}, u32[]{:S(2)}, u32[]{:S(2)}) collective-permute-start(f32[6,288,128]{2,1,0:T(8,128)S(1)} %shard_map.37.refs_0_.refs_1_.own_ref), channel_id=1, source_target_pairs={{0,64},{32,96},{64,128},{96,160},{128,192},{160,224},{192,0},{224,... | collective-permute-start | bytes 2654216 | tf_op jit(solution)/shard_map/ppermute | solution.py:293
  7.5 0.9 copy-start.4
  8.4 36.6 %all-to-all-start = ((f32[32,27,2,128]{3,2,1,0:T(2,128)}), f32[32,27,2,128]{3,2,1,0:T(2,128)S(1)}, u32[]{:S(2)}, u32[]{:S(2)}) async-start(f32[32,27,2,128]{3,2,1,0:T(2,128)} %bitcast.17), calls=%async_computation | async-start | bytes 1769472 | tf_op jit(solution)/shard_map/all_to_all | solution.py:282
  31.4 1.2 copy-start.5
  45.0 0.9 copy-start.2
  45.9 49.1 %all-to-all-start.1 = ((f32[32,27,4,128]{3,2,1,0:T(4,128)}), f32[32,27,4,128]{3,2,1,0:T(4,128)}, u32[]{:S(2)}, u32[]{:S(2)}) async-start(f32[32,27,4,128]{3,2,1,0:T(4,128)} %bitcast.19), calls=%async_computation.1 | async-start | bytes 3538944 | tf_op jit(solution)/shard_map/all_to_all | solution.py:282
  52.1 1.2 copy-start.3
  99.4 1.2 copy-start.1
  100.6 6.3 %copy-start.11 = (s32[8]{0:T(128)S(1)}, s32[8]{0:T(128)}, u32[]{:S(2)}) copy-start(s32[8]{0:T(128)} %param.4) | copy-start | bytes 100
  100.6 49.6 %all-to-all-start.2 = ((f32[32,27,4,128]{3,2,1,0:T(4,128)}), f32[32,27,4,128]{3,2,1,0:T(4,128)}, u32[]{:S(2)}, u32[]{:S(2)}) async-start(f32[32,27,4,128]{3,2,1,0:T(4,128)} %bitcast.15), calls=%async_computation.2 | async-start | bytes 3538944 | tf_op jit(solution)/shard_map/all_to_all | solution.py:282
  155.4 0.9 copy-start.9
  156.3 30.3 %collective-permute-start.2 = (f32[6,288,128]{2,1,0:T(8,128)}, f32[6,288,128]{2,1,0:T(8,128)}, u32[]{:S(2)}, u32[]{:S(2)}) collective-permute-start(f32[6,288,128]{2,1,0:T(8,128)} %get-tuple-element.21), channel_id=1, source_target_pairs={{0,32},{32,64},{64,96},{96,128},{128,160},{160,192},{192,224},{224... | collective-permute-start | bytes 2654216 | tf_op jit(solution)/shard_map/ppermute | solution.py:293
  156.3 30.3 %collective-permute-start.3 = (f32[6,288,128]{2,1,0:T(8,128)}, f32[6,288,128]{2,1,0:T(8,128)}, u32[]{:S(2)}, u32[]{:S(2)}) collective-permute-start(f32[6,288,128]{2,1,0:T(8,128)} %get-tuple-element.22), channel_id=1, source_target_pairs={{0,192},{32,224},{64,0},{96,32},{128,64},{160,96},{192,128},{224,1... | collective-permute-start | bytes 2654216 | tf_op jit(solution)/shard_map/ppermute | solution.py:293
  160.0 31.1 %all-to-all-start.3 = ((f32[32,27,2,128]{3,2,1,0:T(2,128)}), f32[32,27,2,128]{3,2,1,0:T(2,128)S(1)}, u32[]{:S(2)}, u32[]{:S(2)}) async-start(f32[32,27,2,128]{3,2,1,0:T(2,128)} %bitcast.11), calls=%async_computation.3 | async-start | bytes 1769472 | tf_op jit(solution)/shard_map/all_to_all | solution.py:282
  186.7 1.2 copy-start.10
  189.4 0.9 copy-start.7
  191.1 1.2 copy-start.8

commit v3 on v2

--- a/solution.py
+++ b/solution.py
@@ -48,7 +48,7 @@
 
 def terms(table_ref, place):
     start, height, width = place
-    return table_ref[start : start + height, :width], table_ref[start + height : start + 2 * height, :width]
+    return table_ref[start : start + 2 * height, :width]
 
 
 def split(value):
@@ -56,11 +56,22 @@
     return high, (value - high.astype(jnp.float32)).astype(jnp.bfloat16)
 
 
-def product(left, right):
-    def dot(a, b):
-        return jnp.dot(a, b, preferred_element_type=jnp.float32)
-
-    return dot(left[0], right[0]) + (dot(left[0], right[1]) + dot(left[1], right[0]))
+def dot(left, right):
+    return jnp.dot(left, right, preferred_element_type=jnp.float32)
+
+
+def from_left(table, value):
+    height = table.shape[0] // 2
+    high, low = split(value)
+    both = dot(table, high)
+    return both[:height] + (both[height:] + dot(table[:height], low))
+
+
+def from_right(value, table):
+    height, depth = value.shape[0], table.shape[0] // 2
+    high, low = split(value)
+    both = dot(jnp.concatenate([high, low], axis=0), table[:depth])
+    return both[:height] + (both[height:] + dot(high, table[depth:]))
 
 
 def call(kernel, out_shape, flops, size, in_specs, scratch=()):
@@ -128,8 +139,7 @@
             for plane in range(rows):
                 density = own_ref[plane] * guest[plane]
                 mean = jnp.sum(density, keepdims=True) * (1.0 / points)
-                along = product(split(unpack(density - mean, length)), z_table)
-                both = product(y_table, split(along))
+                both = from_left(y_table, from_right(unpack(density - mean, length), z_table))
                 base = number * block + plane
                 for row in range(rows):
                     piece = both[slabs * row : slabs * (row + 1), :LANES]
@@ -171,7 +181,7 @@
                     lines[slab, :rows, first : first + LANES] = in_ref[place : place + rows, :]
             line = lines[:, :, start:stop].reshape(slabs * SLOTS, stop - start)
             total = jnp.sum(line, axis=0, keepdims=True)
-            spectrum = product(x_table, split(line - total * (1.0 / length)))
+            spectrum = from_left(x_table, line - total * (1.0 / length))
             first_row = lax.broadcasted_iota(jnp.int32, spectrum.shape, 0) == 0
             spectrum = spectrum + jnp.where(first_row, total, 0.0)
             scaled = [
@@ -179,7 +189,7 @@
                 for first in range(start, stop, LANES)
             ]
             image = jnp.concatenate(scaled, axis=1)
-            solved = product(back_table, split(image)).reshape(slabs, SLOTS, stop - start)
+            solved = from_left(back_table, image).reshape(slabs, SLOTS, stop - start)
             for first in range(start, stop, LANES):
                 for slab in range(slabs):
                     place = slab * pitch_out + rows * (first // LANES)
@@ -191,42 +201,59 @@
     return work(blocks, kernel_values, entries)
 
 
-def potential_plane(block_ref, place, rows, slabs, y_table, z_table, lower):
+def fields(block_ref, base, rows, slabs, table_ref, places):
     pitch = block_ref.shape[0] // slabs
+    lower = lower_lanes()
+    y_table, z_table = terms(table_ref, places["yt"]), terms(table_ref, places["zt"])
 
     def across(row):
-        return block_ref[pl.ds(place + rows * row, slabs, stride=pitch), :]
-
-    full = jnp.concatenate([across(row) for row in range(rows)], axis=0)
-    parts = []
-    for row in range(rows // 2):
-        shared = across(rows + row)
-        parts.append(jnp.where(lower, shared, 0.0))
-        parts.append(jnp.where(lower, 0.0, shared))
-    wide = jnp.concatenate([full, jnp.concatenate(parts, axis=0)], axis=1)
-    along = product(y_table, split(wide))
-    return pack(product(split(along), z_table))
-
-
-def apply_pairs(blocks, own, guests, weights, table):
+        return block_ref[pl.ds(row, slabs, stride=pitch), :]
+
+    planes = []
+    for plane in range(rows):
+        place = base + plane
+        full = jnp.concatenate([across(place + rows * row) for row in range(rows)], axis=0)
+        parts = []
+        for row in range(rows // 2):
+            shared = across(place + rows * (rows + row))
+            parts.append(jnp.where(lower, shared, 0.0))
+            parts.append(jnp.where(lower, 0.0, shared))
+        wide = jnp.concatenate([full, jnp.concatenate(parts, axis=0)], axis=1)
+        planes.append(pack(from_right(from_left(y_table, wide), z_table)))
+    return planes
+
+
+def sent_back(blocks, count, own, weights, table):
+    places, entries, rows, length = table
+    block = rows * rows * length // LANES
+
+    def kernel(weight, block_ref, own_ref, table_ref, *sent):
+        for number in range(count):
+            made = fields(block_ref, number * block, rows, length // rows, table_ref, places)
+            for plane, field in enumerate(made):
+                sent[number][plane] = (weight[0] * own_ref[plane]) * field
+
+    shape = packed_shape(rows, length)
+    work = call(kernel, [shape] * count, count * 12 * length**3 * rows, count * 2**22, [SMEM] + [VMEM] * 3)
+    return work(weights, blocks, own, entries)
+
+
+def guest_terms(blocks, guests, weights, table):
     places, entries, rows, length = table
     count = len(guests)
     block = rows * rows * length // LANES
 
-    def kernel(weight, block_ref, own_ref, *refs):
-        guest_refs, table_ref, total, sent = refs[:count], refs[count], refs[count + 1], refs[count + 2 :]
-        lower = lower_lanes()
-        y_table, z_table = terms(table_ref, places["yt"]), terms(table_ref, places["zt"])
-        for number in range(count):
-            for plane in range(rows):
-                field = potential_plane(block_ref, number * block + plane, rows, length // rows, y_table, z_table, lower)
-                term = (weight[number + 1] * guest_refs[number][plane]) * field
+    def kernel(weight, block_ref, *refs):
+        guest_refs, table_ref, total = refs[:count], refs[count], refs[count + 1]
+        for number, guest in enumerate(guest_refs):
+            made = fields(block_ref, number * block, rows, length // rows, table_ref, places)
+            for plane, field in enumerate(made):
+                term = (weight[number + 1] * guest[plane]) * field
                 total[plane] = term if number == 0 else total[plane] + term
-                sent[number][plane] = (weight[0] * own_ref[plane]) * field
 
     shape = packed_shape(rows, length)
-    work = call(kernel, [shape] * (1 + count), count * 12 * length**3 * rows, count * 2**22, [SMEM] + [VMEM] * (3 + count))
-    return work(weights, blocks, own, *guests, entries)
+    work = call(kernel, shape, count * 12 * length**3 * rows, count * 2**22, [SMEM] + [VMEM] * (2 + count))
+    return work(weights, blocks, *guests, entries)
 
 
 def add_received(partial, received):
@@ -244,10 +271,7 @@
     places, entries, rows, length = table
 
     def kernel(weight, block_ref, own_ref, other, table_ref, out):
-        lower = lower_lanes()
-        y_table, z_table = terms(table_ref, places["yt"]), terms(table_ref, places["zt"])
-        for plane in range(rows):
-            field = potential_plane(block_ref, plane, rows, length // rows, y_table, z_table, lower)
+        for plane, field in enumerate(fields(block_ref, 0, rows, length // rows, table_ref, places)):
             out[plane] = -unpack(other[plane] + (weight[0] * own_ref[plane]) * field, length)
 
     shape = jax.ShapeDtypeStruct((rows, length, length), jnp.float32)
@@ -307,7 +331,8 @@
     pair_back = exchange(middle(pair_lines, [0, 1], kernel_values, table))
     own_image, pair_back = lax.optimization_barrier((own_image, pair_back))
     own_back = exchange(own_image)
-    partial, to_next, to_far = apply_pairs(pair_back, own, guests, weights, table)
+    to_next, to_far = sent_back(pair_back, len(guests), own, weights, table)
+    partial = guest_terms(pair_back, guests, weights, table)
     received = [shifted(to_next, 1), shifted(to_far, -2)]
     others = add_received(partial, received)
     return apply_own(own_back, own, others, weights, table)[None]

time: 196 us -> 194 us (0.990)
  Pallas kernels: 22.2 us -> 25.9 us
  waiting for transfers between devices: 122 us -> 119 us
  local copies, waits for them, and re-layouts: 11.6 us -> 9.5 us
    ppermute x4, waiting for transfers between devices: 27.4 us -> 23.1 us  [shifted(): lax.ppermute(array, 'band', [(group, (group + by) % groups) for group in...]
    pallas_call x1 -> x2, Pallas kernels: 5.22 us -> 8.94 us  [the longest x1 4.69 us: sent_back(): return work(weights, blocks, own, entries)]
    unnamed x24 -> x20, local copies, waits for them, and re-layouts: 11 us -> 8.86 us
  transfers between devices with their start and end apart: 8 -> 8, of which waited for: 7 -> 7; matrix products, arithmetic and copies ran while one was open for 1% -> 1% of each run, Pallas kernels for 5% -> 7%
where the time goes in v3:
time: 194 us; the launch traced here: 193 us
  waiting for transfers between devices  119 us (61%)
  starting transfers between devices  38.5 us (20%)
  Pallas kernels  25.9 us (13%)
  local copies, waits for them, and re-layouts  9.5 us (5%)
    all_to_all x4, waiting for transfers between devices, exchange(): lax.all_to_all(cut, 'space', split_axis=0, concat_axis=0, tiled=True)  95.9 us
    all_to_all x4, starting transfers between devices, exchange(): lax.all_to_all(cut, 'space', split_axis=0, concat_axis=0, tiled=True)  30.4 us
    ppermute x4, waiting for transfers between devices, shifted(): lax.ppermute(array, 'band', [(group, (group + by) % groups) for group in...  23.1 us
    unnamed x20, local copies, waits for them, and re-layouts  8.86 us
    ppermute x4, starting transfers between devices, shifted(): lax.ppermute(array, 'band', [(group, (group + by) % groups) for group in...  8.06 us
    pallas_call x2, Pallas kernels, middle(): return work(blocks, kernel_values, entries)  6.8 us
    pallas_call x2, Pallas kernels, forward(): return work(own, *guests, entries)  5.5 us
    pallas_call x1, Pallas kernels, sent_back(): return work(weights, blocks, own, entries)  4.69 us
  transfers between devices with their start and end apart: 8, of which 7 were waited for; matrix products, arithmetic and copies ran while one was open for 1% of the time, Pallas kernels for 7%

profile of v3, /device:TPU:1, one launch (start us, length us, event | category | flops | bytes accessed | tf_op | source)
XLA Modules:
  0.0 193.5 jit_solution(1787190334803659899)
XLA Ops:
  0.0 1.4 copy-done.6
  1.4 0.1 shard_map.37.refs_0_.refs_1_.own_ref
  1.5 4.4 %collective-permute-start = (f32[6,288,128]{2,1,0:T(8,128)S(1)}, f32[6,288,128]{2,1,0:T(8,128)}, u32[]{:S(2)}, u32[]{:S(2)}) collective-permute-start(f32[6,288,128]{2,1,0:T(8,128)S(1)} %shard_map.37.refs_0_.refs_1_.own_ref), channel_id=1, source_target_pairs={{0,224},{32,0},{64,32},{96,64},{128,96},{160,128},{192,160},{224,1... | collective-permute-start | bytes 2654216 | tf_op jit(solution)/shard_map/ppermute | solution.py:317
  5.9 1.5 shard_map.39
  7.5 0.9 copy-done.4
  8.4 11.9 %all-to-all-start = ((f32[32,27,2,128]{3,2,1,0:T(2,128)}), f32[32,27,2,128]{3,2,1,0:T(2,128)S(1)}, u32[]{:S(2)}, u32[]{:S(2)}) async-start(f32[32,27,2,128]{3,2,1,0:T(2,128)} %bitcast.17), calls=%async_computation | async-start | bytes 1769472 | tf_op jit(solution)/shard_map/all_to_all | solution.py:306
  20.3 3.9 %collective-permute-done.refs_1_.refs_0_ = f32[6,288,128]{2,1,0:T(8,128)} collective-permute-done((f32[6,288,128]{2,1,0:T(8,128)S(1)}, f32[6,288,128]{2,1,0:T(8,128)}, u32[]{:S(2)}, u32[]{:S(2)}) %collective-permute-start) | collective-permute-done | bytes 884768 | tf_op jit(solution)/shard_map/ppermute | solution.py:317
  24.2 3.2 %collective-permute-done.1.refs_2_.refs_1_ = f32[6,288,128]{2,1,0:T(8,128)} collective-permute-done((f32[6,288,128]{2,1,0:T(8,128)S(1)}, f32[6,288,128]{2,1,0:T(8,128)}, u32[]{:S(2)}, u32[]{:S(2)}) %collective-permute-start.1) | collective-permute-done | bytes 884768 | tf_op jit(solution)/shard_map/ppermute | solution.py:317
  27.4 4.0 %shard_map.38 = f32[3456,128]{1,0:T(8,128)S(1)} custom-call(f32[6,288,128]{2,1,0:T(8,128)S(1)} %shard_map.37.refs_0_.refs_1_.own_ref, f32[6,288,128]{2,1,0:T(8,128)} %collective-permute-done.refs_1_.refs_0_, f32[6,288,128]{2,1,0:T(8,128)} %collective-permute-done.1.refs_2_.refs_1_, bf16[2560,256]{1,0:T(8,128)(2,1)S(1)} %copy-done), custom_call_target="tpu_custom_call" | custom-call | flops 16307453952 | bytes 8388608 | tf_op jit(solution)/shard_map/pallas_call | solution.py:157
  31.4 1.2 copy-done.5
  32.6 12.4 %all-to-all-done = f32[32,27,2,128]{3,2,1,0:T(2,128)S(1)} async-done(((f32[32,27,2,128]{3,2,1,0:T(2,128)}), f32[32,27,2,128]{3,2,1,0:T(2,128)S(1)}, u32[]{:S(2)}, u32[]{:S(2)}) %all-to-all-start) | async-done | bytes 884768 | tf_op jit(solution)/shard_map/all_to_all | solution.py:306
  45.0 0.9 copy-done.2
  45.9 5.8 %all-to-all-start.1 = ((f32[32,27,4,128]{3,2,1,0:T(4,128)}), f32[32,27,4,128]{3,2,1,0:T(4,128)}, u32[]{:S(2)}, u32[]{:S(2)}) async-start(f32[32,27,4,128]{3,2,1,0:T(4,128)} %bitcast.19), calls=%async_computation.1 | async-start | bytes 3538944 | tf_op jit(solution)/shard_map/all_to_all | solution.py:306
  51.7 0.3 select_multiply_fusion.values
  52.1 1.2 copy-done.3
  53.2 2.7 %shard_map.40 = f32[1728,128]{1,0:T(8,128)} custom-call(f32[1728,128]{1,0:T(8,128)S(1)} %bitcast.16, f32[192,1152]{1,0:T(8,128)S(1)} %select_multiply_fusion.values, bf16[2560,256]{1,0:T(8,128)(2,1)S(1)} %copy-done), custom_call_target="tpu_custom_call" | custom-call | flops 509607936 | bytes 4718592 | tf_op jit(solution)/shard_map/pallas_call | solution.py:201
  56.0 39.0 %all-to-all-done.1 = f32[32,27,4,128]{3,2,1,0:T(4,128)} async-done(((f32[32,27,4,128]{3,2,1,0:T(4,128)}), f32[32,27,4,128]{3,2,1,0:T(4,128)}, u32[]{:S(2)}, u32[]{:S(2)}) %all-to-all-start.1) | async-done | bytes 1769504 | tf_op jit(solution)/shard_map/all_to_all | solution.py:306
  95.0 4.1 %shard_map.41 = f32[3456,128]{1,0:T(8,128)S(1)} custom-call(f32[3456,128]{1,0:T(8,128)} %bitcast.8.in_ref, f32[192,1152]{1,0:T(8,128)S(1)} %select_multiply_fusion.values, bf16[2560,256]{1,0:T(8,128)(2,1)S(1)} %copy-done), custom_call_target="tpu_custom_call" | custom-call | flops 1019215872 | bytes 9437184 | tf_op jit(solution)/shard_map/pallas_call | solution.py:201
  99.1 1.2 copy-done.1
  100.3 6.3 %all-to-all-start.2 = ((f32[32,27,4,128]{3,2,1,0:T(4,128)}), f32[32,27,4,128]{3,2,1,0:T(4,128)}, u32[]{:S(2)}, u32[]{:S(2)}) async-start(f32[32,27,4,128]{3,2,1,0:T(4,128)} %bitcast.15), calls=%async_computation.2 | async-start | bytes 3538944 | tf_op jit(solution)/shard_map/all_to_all | solution.py:306
  106.7 0.6 gather_fusion
  107.4 42.5 %all-to-all-done.2 = f32[32,27,4,128]{3,2,1,0:T(4,128)} async-done(((f32[32,27,4,128]{3,2,1,0:T(4,128)}), f32[32,27,4,128]{3,2,1,0:T(4,128)}, u32[]{:S(2)}, u32[]{:S(2)}) %all-to-all-start.2) | async-done | bytes 1769504 | tf_op jit(solution)/shard_map/all_to_all | solution.py:306
  149.9 4.7 %shard_map.43 = (f32[6,288,128]{2,1,0:T(8,128)}, f32[6,288,128]{2,1,0:T(8,128)}) custom-call(f32[3]{0:T(128)S(1)} %gather_fusion, f32[3456,128]{1,0:T(8,128)} %bitcast.10.block_ref, f32[6,288,128]{2,1,0:T(8,128)S(1)} %shard_map.37.refs_0_.refs_1_.own_ref, bf16[2560,256]{1,0:T(8,128)(2,1)S(1)} %copy-done), custom_call_target="tpu_custom_call" | custom-call | flops 1019215872 | bytes 8388608 | tf_op jit(solution)/shard_map/pallas_call | solution.py:238
  154.5 3.7 %collective-permute-start.3 = (f32[6,288,128]{2,1,0:T(8,128)}, f32[6,288,128]{2,1,0:T(8,128)}, u32[]{:S(2)}, u32[]{:S(2)}) collective-permute-start(f32[6,288,128]{2,1,0:T(8,128)} %get-tuple-element.20), channel_id=1, source_target_pairs={{0,192},{32,224},{64,0},{96,32},{128,64},{160,96},{192,128},{224,1... | collective-permute-start | bytes 2654216 | tf_op jit(solution)/shard_map/ppermute | solution.py:317
  158.2 6.4 %all-to-all-start.3 = ((f32[32,27,2,128]{3,2,1,0:T(2,128)}), f32[32,27,2,128]{3,2,1,0:T(2,128)S(1)}, u32[]{:S(2)}, u32[]{:S(2)}) async-start(f32[32,27,2,128]{3,2,1,0:T(2,128)} %bitcast.11), calls=%async_computation.3 | async-start | bytes 1769472 | tf_op jit(solution)/shard_map/all_to_all | solution.py:306
  164.7 4.3 %shard_map.42.part = f32[6,288,128]{2,1,0:T(8,128)S(1)} custom-call(f32[3]{0:T(128)S(1)} %gather_fusion, f32[3456,128]{1,0:T(8,128)} %bitcast.10.block_ref, f32[6,288,128]{2,1,0:T(8,128)} %collective-permute-done.refs_1_.refs_0_, f32[6,288,128]{2,1,0:T(8,128)} %collective-permute-done.1.refs_2_.refs_1_, bf16[2560,256]{1,0:T(8,128)(2,1)S(1)} %copy-done), custom_call_target="tpu_custom_call" | custom-call | flops 1019215872 | bytes 8388608 | tf_op jit(solution)/shard_map/pallas_call | solution.py:256
  168.9 16.0 %collective-permute-done.2.first = f32[6,288,128]{2,1,0:T(8,128)} collective-permute-done((f32[6,288,128]{2,1,0:T(8,128)}, f32[6,288,128]{2,1,0:T(8,128)}, u32[]{:S(2)}, u32[]{:S(2)}) %collective-permute-start.2) | collective-permute-done | bytes 884768 | tf_op jit(solution)/shard_map/ppermute | solution.py:317
  184.9 1.6 shard_map.44.other
  186.4 0.9 copy-done.7
  187.4 2.0 %all-to-all-done.3 = f32[32,27,2,128]{3,2,1,0:T(2,128)S(1)} async-done(((f32[32,27,2,128]{3,2,1,0:T(2,128)}), f32[32,27,2,128]{3,2,1,0:T(2,128)S(1)}, u32[]{:S(2)}, u32[]{:S(2)}) %all-to-all-start.3) | async-done | bytes 884768 | tf_op jit(solution)/shard_map/all_to_all | solution.py:306
  189.3 1.2 copy-done.8
  190.5 3.0 %shard_map.45 = f32[6,192,192]{2,1,0:T(8,128)} custom-call(f32[3]{0:T(128)S(1)} %gather_fusion, f32[1728,128]{1,0:T(8,128)S(1)} %bitcast.18, f32[6,288,128]{2,1,0:T(8,128)S(1)} %shard_map.37.refs_0_.refs_1_.own_ref, f32[6,288,128]{2,1,0:T(8,128)S(1)} %copy-done.8, bf16[2560,256]{1,0:T(8,128)(2,1)S(1)} %copy-done), custom_call_target="tpu_custom_call" | custom-call | flops 509607936 | bytes 4194304 | tf_op jit(solution)/shard_map/pallas_call | solution.py:279
  (22 shorter events, 0.1 us)
Async XLA Ops:
  0.0 5.9 %copy-start = (bf16[2560,256]{1,0:T(8,128)(2,1)S(1)}, bf16[2560,256]{1,0:T(8,128)(2,1)}, u32[]{:S(2)}) copy-start(bf16[2560,256]{1,0:T(8,128)(2,1)} %constant.104.clone.refs_3_.refs_2_.table_ref) | copy-start | bytes 3932164
  0.0 1.4 copy-start.6
  1.5 22.7 %collective-permute-start = (f32[6,288,128]{2,1,0:T(8,128)S(1)}, f32[6,288,128]{2,1,0:T(8,128)}, u32[]{:S(2)}, u32[]{:S(2)}) collective-permute-start(f32[6,288,128]{2,1,0:T(8,128)S(1)} %shard_map.37.refs_0_.refs_1_.own_ref), channel_id=1, source_target_pairs={{0,224},{32,0},{64,32},{96,64},{128,96},{160,128},{192,160},{224,1... | collective-permute-start | bytes 2654216 | tf_op jit(solution)/shard_map/ppermute | solution.py:317
  5.9 21.5 %collective-permute-start.1 = (f32[6,288,128]{2,1,0:T(8,128)S(1)}, f32[6,288,128]{2,1,0:T(8,128)}, u32[]{:S(2)}, u32[]{:S(2)}) collective-permute-start(f32[6,288,128]{2,1,0:T(8,128)S(1)} %shard_map.37.refs_0_.refs_1_.own_ref), channel_id=1, source_target_pairs={{0,64},{32,96},{64,128},{96,160},{128,192},{160,224},{192,0},{224,... | collective-permute-start | bytes 2654216 | tf_op jit(solution)/shard_map/ppermute | solution.py:317
  7.5 0.9 copy-start.4
  8.4 36.6 %all-to-all-start = ((f32[32,27,2,128]{3,2,1,0:T(2,128)}), f32[32,27,2,128]{3,2,1,0:T(2,128)S(1)}, u32[]{:S(2)}, u32[]{:S(2)}) async-start(f32[32,27,2,128]{3,2,1,0:T(2,128)} %bitcast.17), calls=%async_computation | async-start | bytes 1769472 | tf_op jit(solution)/shard_map/all_to_all | solution.py:306
  31.4 1.2 copy-start.5
  45.0 0.9 copy-start.2
  45.9 49.1 %all-to-all-start.1 = ((f32[32,27,4,128]{3,2,1,0:T(4,128)}), f32[32,27,4,128]{3,2,1,0:T(4,128)}, u32[]{:S(2)}, u32[]{:S(2)}) async-start(f32[32,27,4,128]{3,2,1,0:T(4,128)} %bitcast.19), calls=%async_computation.1 | async-start | bytes 3538944 | tf_op jit(solution)/shard_map/all_to_all | solution.py:306
  52.1 1.2 copy-start.3
  99.1 1.2 copy-start.1
  100.3 6.3 %copy-start.9 = (s32[8]{0:T(128)S(1)}, s32[8]{0:T(128)}, u32[]{:S(2)}) copy-start(s32[8]{0:T(128)} %param.4) | copy-start | bytes 100
  100.3 49.6 %all-to-all-start.2 = ((f32[32,27,4,128]{3,2,1,0:T(4,128)}), f32[32,27,4,128]{3,2,1,0:T(4,128)}, u32[]{:S(2)}, u32[]{:S(2)}) async-start(f32[32,27,4,128]{3,2,1,0:T(4,128)} %bitcast.15), calls=%async_computation.2 | async-start | bytes 3538944 | tf_op jit(solution)/shard_map/all_to_all | solution.py:306
  154.5 30.3 %collective-permute-start.2 = (f32[6,288,128]{2,1,0:T(8,128)}, f32[6,288,128]{2,1,0:T(8,128)}, u32[]{:S(2)}, u32[]{:S(2)}) collective-permute-start(f32[6,288,128]{2,1,0:T(8,128)} %get-tuple-element.19), channel_id=1, source_target_pairs={{0,32},{32,64},{64,96},{96,128},{128,160},{160,192},{192,224},{224... | collective-permute-start | bytes 2654216 | tf_op jit(solution)/shard_map/ppermute | solution.py:317
  154.5 30.3 %collective-permute-start.3 = (f32[6,288,128]{2,1,0:T(8,128)}, f32[6,288,128]{2,1,0:T(8,128)}, u32[]{:S(2)}, u32[]{:S(2)}) collective-permute-start(f32[6,288,128]{2,1,0:T(8,128)} %get-tuple-element.20), channel_id=1, source_target_pairs={{0,192},{32,224},{64,0},{96,32},{128,64},{160,96},{192,128},{224,1... | collective-permute-start | bytes 2654216 | tf_op jit(solution)/shard_map/ppermute | solution.py:317
  158.2 31.1 %all-to-all-start.3 = ((f32[32,27,2,128]{3,2,1,0:T(2,128)}), f32[32,27,2,128]{3,2,1,0:T(2,128)S(1)}, u32[]{:S(2)}, u32[]{:S(2)}) async-start(f32[32,27,2,128]{3,2,1,0:T(2,128)} %bitcast.11), calls=%async_computation.3 | async-start | bytes 1769472 | tf_op jit(solution)/shard_map/all_to_all | solution.py:306
  186.4 0.9 copy-start.7
  189.3 1.2 copy-start.8

commit v4 on v3

--- a/solution.py
+++ b/solution.py
@@ -14,6 +14,7 @@
 SLOTS = 8
 VMEM = pl.BlockSpec(memory_space=pltpu.VMEM)
 SMEM = pl.BlockSpec(memory_space=pltpu.SMEM)
+ANY = pl.BlockSpec(memory_space=pltpu.HBM)
 
 
 def tables(length, slabs, rows):
@@ -168,9 +169,12 @@
 
     pitch_in, pitch_out = blocks.shape[0] // slabs, block_pitch(len(pairs) * depth)
 
-    def kernel(in_ref, values, table_ref, out, lines):
+    def kernel(source, values, table_ref, out, lines, in_ref, arrived):
+        transfer = pltpu.make_async_copy(source, in_ref, arrived)
+        transfer.start()
         lines[:, rows:, :] = jnp.zeros((slabs, SLOTS - rows, lanes), jnp.float32)
         x_table, back_table = terms(table_ref, places["x"]), terms(table_ref, places["xt"])
+        transfer.wait()
         for start in range(0, lanes, tile):
             stop = min(start + tile, lanes)
             for first in range(start, stop, LANES):
@@ -196,9 +200,13 @@
                     out[place : place + rows, :] = solved[slab, :rows, first - start : first - start + LANES]
 
     shape = jax.ShapeDtypeStruct((slabs * pitch_out, LANES), jnp.float32)
-    scratch = [pltpu.VMEM((slabs, SLOTS, lanes), jnp.float32)]
-    work = call(kernel, shape, lanes * 12 * length * length, lanes * 2**12, [VMEM] * 3, scratch)
-    return work(blocks, kernel_values, entries)
+    scratch = [
+        pltpu.VMEM((slabs, SLOTS, lanes), jnp.float32),
+        pltpu.VMEM(blocks.shape, jnp.float32),
+        pltpu.SemaphoreType.DMA(()),
+    ]
+    work = call(kernel, shape, lanes * 12 * length * length, lanes * 2**12, [ANY, VMEM, VMEM], scratch)
+    return work(pltpu.with_memory_space_constraint(blocks, pltpu.HBM), kernel_values, entries)
 
 
 def fields(block_ref, base, rows, slabs, table_ref, places):
@@ -270,12 +278,18 @@
 def apply_own(blocks, own, others, weights, table):
     places, entries, rows, length = table
 
-    def kernel(weight, block_ref, own_ref, other, table_ref, out):
-        for plane, field in enumerate(fields(block_ref, 0, rows, length // rows, table_ref, places)):
-            out[plane] = -unpack(other[plane] + (weight[0] * own_ref[plane]) * field, length)
+    def kernel(weight, block_ref, own_ref, other, table_ref, out, held, arrived):
+        transfer = pltpu.make_async_copy(other, held, arrived)
+        transfer.start()
+        made = fields(block_ref, 0, rows, length // rows, table_ref, places)
+        transfer.wait()
+        for plane, field in enumerate(made):
+            out[plane] = -unpack(held[plane] + (weight[0] * own_ref[plane]) * field, length)
 
     shape = jax.ShapeDtypeStruct((rows, length, length), jnp.float32)
-    work = call(kernel, shape, 12 * length**3 * rows, 2**22, [SMEM] + [VMEM] * 4)
+    scratch = [pltpu.VMEM(others.shape, jnp.float32), pltpu.SemaphoreType.DMA(())]
+    work = call(kernel, shape, 12 * length**3 * rows, 2**22, [SMEM, VMEM, VMEM, ANY, VMEM], scratch)
+    others = pltpu.with_memory_space_constraint(others, pltpu.HBM)
     return work(weights, blocks, own, others, entries)
 
 

time: 194 us -> 193 us (level)
  local copies, waits for them, and re-layouts: 9.5 us -> 6.53 us
  Pallas kernels: 25.9 us -> 28.2 us
    unnamed x20 -> x16, local copies, waits for them, and re-layouts: 8.86 us -> 5.89 us
  transfers between devices with their start and end apart: 8 -> 8, of which waited for: 7 -> 7; matrix products, arithmetic and copies ran while one was open for 1% -> 1% of each run, Pallas kernels for 7% -> 8%
where the time goes in v4:
time: 193 us; the launch traced here: 192 us
  waiting for transfers between devices  118 us (61%)
  starting transfers between devices  38.5 us (20%)
  Pallas kernels  28.2 us (15%)
  local copies, waits for them, and re-layouts  6.53 us (3%)
    all_to_all x4, waiting for transfers between devices, exchange(): lax.all_to_all(cut, 'space', split_axis=0, concat_axis=0, tiled=True)  96.2 us
    all_to_all x4, starting transfers between devices, exchange(): lax.all_to_all(cut, 'space', split_axis=0, concat_axis=0, tiled=True)  30.5 us
    ppermute x4, waiting for transfers between devices, shifted(): lax.ppermute(array, 'band', [(group, (group + by) % groups) for group in...  22.1 us
    ppermute x4, starting transfers between devices, shifted(): lax.ppermute(array, 'band', [(group, (group + by) % groups) for group in...  8.06 us
    pallas_call x2, Pallas kernels, middle(): work(pltpu.with_memory_space_constraint(blocks, pltpu.HBM), kernel_values...  7.78 us
    pallas_call x2, Pallas kernels, forward(): return work(own, *guests, entries)  6.15 us
    unnamed x16, local copies, waits for them, and re-layouts  5.89 us
    pallas_call x1, Pallas kernels, sent_back(): return work(weights, blocks, own, entries)  4.68 us
  transfers between devices with their start and end apart: 8, of which 7 were waited for; matrix products, arithmetic and copies ran while one was open for 1% of the time, Pallas kernels for 8%

profile of v4, /device:TPU:1, one launch (start us, length us, event | category | flops | bytes accessed | tf_op | source)
XLA Modules:
  0.0 192.4 jit_solution(15441859271279201462)
XLA Ops:
  0.0 1.4 copy-done.3
  1.4 0.1 shard_map.37.refs_0_.refs_1_.own_ref
  1.5 4.4 %collective-permute-start = (f32[6,288,128]{2,1,0:T(8,128)S(1)}, f32[6,288,128]{2,1,0:T(8,128)S(1)}, u32[]{:S(2)}, u32[]{:S(2)}) collective-permute-start(f32[6,288,128]{2,1,0:T(8,128)S(1)} %shard_map.37.refs_0_.refs_1_.own_ref), channel_id=1, source_target_pairs={{0,224},{32,0},{64,32},{96,64},{128,96},{160,128},{192,160},{224,1... | collective-permute-start | bytes 2654216 | tf_op jit(solution)/shard_map/ppermute | solution.py:331
  5.9 0.0 collective-permute-start.1
  5.9 2.5 %shard_map.39 = f32[1728,128]{1,0:T(8,128)} custom-call(f32[6,288,128]{2,1,0:T(8,128)S(1)} %shard_map.37.refs_0_.refs_1_.own_ref, f32[6,288,128]{2,1,0:T(8,128)S(1)} %shard_map.37.refs_0_.refs_1_.own_ref, bf16[2560,256]{1,0:T(8,128)(2,1)S(1)} %copy-done), custom_call_target="tpu_custom_call" | custom-call | flops 509607936 | bytes 4194304 | tf_op jit(solution)/shard_map/pallas_call | solution.py:158
  8.4 12.0 %all-to-all-start = ((f32[32,27,2,128]{3,2,1,0:T(2,128)}), f32[32,27,2,128]{3,2,1,0:T(2,128)}, u32[]{:S(2)}, u32[]{:S(2)}) async-start(f32[32,27,2,128]{3,2,1,0:T(2,128)} %bitcast.5), calls=%async_computation | async-start | bytes 1769472 | tf_op jit(solution)/shard_map/all_to_all | solution.py:320
  20.4 3.9 %collective-permute-done.refs_1_.refs_0_ = f32[6,288,128]{2,1,0:T(8,128)S(1)} collective-permute-done((f32[6,288,128]{2,1,0:T(8,128)S(1)}, f32[6,288,128]{2,1,0:T(8,128)S(1)}, u32[]{:S(2)}, u32[]{:S(2)}) %collective-permute-start) | collective-permute-done | bytes 884768 | tf_op jit(solution)/shard_map/ppermute | solution.py:331
  24.2 3.2 %collective-permute-done.1.refs_2_.refs_1_ = f32[6,288,128]{2,1,0:T(8,128)} collective-permute-done((f32[6,288,128]{2,1,0:T(8,128)S(1)}, f32[6,288,128]{2,1,0:T(8,128)}, u32[]{:S(2)}, u32[]{:S(2)}) %collective-permute-start.1) | collective-permute-done | bytes 884768 | tf_op jit(solution)/shard_map/ppermute | solution.py:331
  27.4 3.7 %shard_map.38 = f32[3456,128]{1,0:T(8,128)S(1)} custom-call(f32[6,288,128]{2,1,0:T(8,128)S(1)} %shard_map.37.refs_0_.refs_1_.own_ref, f32[6,288,128]{2,1,0:T(8,128)S(1)} %collective-permute-done.refs_1_.refs_0_, f32[6,288,128]{2,1,0:T(8,128)} %collective-permute-done.1.refs_2_.refs_1_, bf16[2560,256]{1,0:T(8,128)(2,1)S(1)} %copy-done), custom_call_target="tpu_custom_call" | custom-call | flops 16307453952 | bytes 8388608 | tf_op jit(solution)/shard_map/pallas_call | solution.py:158
  31.2 1.2 copy-done.2
  32.4 12.7 %all-to-all-done = f32[32,27,2,128]{3,2,1,0:T(2,128)} async-done(((f32[32,27,2,128]{3,2,1,0:T(2,128)}), f32[32,27,2,128]{3,2,1,0:T(2,128)}, u32[]{:S(2)}, u32[]{:S(2)}) %all-to-all-start) | async-done | bytes 884768 | tf_op jit(solution)/shard_map/all_to_all | solution.py:320
  45.1 5.8 %all-to-all-start.1 = ((f32[32,27,4,128]{3,2,1,0:T(4,128)}), f32[32,27,4,128]{3,2,1,0:T(4,128)}, u32[]{:S(2)}, u32[]{:S(2)}) async-start(f32[32,27,4,128]{3,2,1,0:T(4,128)} %bitcast.17), calls=%async_computation.1 | async-start | bytes 3538944 | tf_op jit(solution)/shard_map/all_to_all | solution.py:320
  50.9 0.3 select_multiply_fusion.values
  51.3 3.8 %shard_map.40 = f32[1728,128]{1,0:T(8,128)} custom-call(f32[1728,128]{1,0:T(8,128)} %bitcast.6.source, f32[192,1152]{1,0:T(8,128)S(1)} %select_multiply_fusion.values, bf16[2560,256]{1,0:T(8,128)(2,1)S(1)} %copy-done), custom_call_target="tpu_custom_call" | custom-call | flops 509607936 | bytes 4718592 | tf_op jit(solution)/shard_map/pallas_call | solution.py:209
  55.1 39.1 %all-to-all-done.1 = f32[32,27,4,128]{3,2,1,0:T(4,128)} async-done(((f32[32,27,4,128]{3,2,1,0:T(4,128)}), f32[32,27,4,128]{3,2,1,0:T(4,128)}, u32[]{:S(2)}, u32[]{:S(2)}) %all-to-all-start.1) | async-done | bytes 1769504 | tf_op jit(solution)/shard_map/all_to_all | solution.py:320
  94.2 3.9 %shard_map.41 = f32[3456,128]{1,0:T(8,128)S(1)} custom-call(f32[3456,128]{1,0:T(8,128)} %bitcast.8.source, f32[192,1152]{1,0:T(8,128)S(1)} %select_multiply_fusion.values, bf16[2560,256]{1,0:T(8,128)(2,1)S(1)} %copy-done), custom_call_target="tpu_custom_call" | custom-call | flops 1019215872 | bytes 9437184 | tf_op jit(solution)/shard_map/pallas_call | solution.py:209
  98.2 1.2 copy-done.1
  99.4 6.3 %all-to-all-start.2 = ((f32[32,27,4,128]{3,2,1,0:T(4,128)}), f32[32,27,4,128]{3,2,1,0:T(4,128)}, u32[]{:S(2)}, u32[]{:S(2)}) async-start(f32[32,27,4,128]{3,2,1,0:T(4,128)} %bitcast.15), calls=%async_computation.2 | async-start | bytes 3538944 | tf_op jit(solution)/shard_map/all_to_all | solution.py:320
  105.7 0.1 fusion.19
  105.8 0.6 gather_fusion
  106.5 42.5 %all-to-all-done.2 = f32[32,27,4,128]{3,2,1,0:T(4,128)} async-done(((f32[32,27,4,128]{3,2,1,0:T(4,128)}), f32[32,27,4,128]{3,2,1,0:T(4,128)}, u32[]{:S(2)}, u32[]{:S(2)}) %all-to-all-start.2) | async-done | bytes 1769504 | tf_op jit(solution)/shard_map/all_to_all | solution.py:320
  148.9 4.7 %shard_map.43 = (f32[6,288,128]{2,1,0:T(8,128)}, f32[6,288,128]{2,1,0:T(8,128)}) custom-call(f32[3]{0:T(128)S(1)} %gather_fusion, f32[3456,128]{1,0:T(8,128)} %bitcast.10.block_ref, f32[6,288,128]{2,1,0:T(8,128)S(1)} %shard_map.37.refs_0_.refs_1_.own_ref, bf16[2560,256]{1,0:T(8,128)(2,1)S(1)} %copy-done), custom_call_target="tpu_custom_call" | custom-call | flops 1019215872 | bytes 8388608 | tf_op jit(solution)/shard_map/pallas_call | solution.py:246
  153.6 0.0 collective-permute-start.2
  153.6 3.7 %collective-permute-start.3 = (f32[6,288,128]{2,1,0:T(8,128)}, f32[6,288,128]{2,1,0:T(8,128)}, u32[]{:S(2)}, u32[]{:S(2)}) collective-permute-start(f32[6,288,128]{2,1,0:T(8,128)} %get-tuple-element.20), channel_id=1, source_target_pairs={{0,192},{32,224},{64,0},{96,32},{128,64},{160,96},{192,128},{224,1... | collective-permute-start | bytes 2654216 | tf_op jit(solution)/shard_map/ppermute | solution.py:331
  157.3 6.4 %all-to-all-start.3 = ((f32[32,27,2,128]{3,2,1,0:T(2,128)}), f32[32,27,2,128]{3,2,1,0:T(2,128)S(1)}, u32[]{:S(2)}, u32[]{:S(2)}) async-start(f32[32,27,2,128]{3,2,1,0:T(2,128)} %bitcast.11), calls=%async_computation.3 | async-start | bytes 1769472 | tf_op jit(solution)/shard_map/all_to_all | solution.py:320
  163.7 1.2 copy-done.5
  164.9 4.0 %shard_map.42.part = f32[6,288,128]{2,1,0:T(8,128)S(1)} custom-call(f32[3]{0:T(128)S(1)} %gather_fusion, f32[3456,128]{1,0:T(8,128)} %bitcast.10.block_ref, f32[6,288,128]{2,1,0:T(8,128)S(1)} %copy-done.5, f32[6,288,128]{2,1,0:T(8,128)} %collective-permute-done.1.refs_2_.refs_1_, bf16[2560,256]{1,0:T(8,128)(2,1)S(1)} %copy-done), custom_call_target="tpu_custom_call" | custom-call | flops 1019215872 | bytes 8388608 | tf_op jit(solution)/shard_map/pallas_call | solution.py:264
  168.9 15.1 %collective-permute-done.2.first = f32[6,288,128]{2,1,0:T(8,128)} collective-permute-done((f32[6,288,128]{2,1,0:T(8,128)}, f32[6,288,128]{2,1,0:T(8,128)}, u32[]{:S(2)}, u32[]{:S(2)}) %collective-permute-start.2) | collective-permute-done | bytes 884768 | tf_op jit(solution)/shard_map/ppermute | solution.py:331
  184.0 1.6 shard_map.44.other
  185.5 0.9 copy-done.6
  186.4 2.0 %all-to-all-done.3 = f32[32,27,2,128]{3,2,1,0:T(2,128)S(1)} async-done(((f32[32,27,2,128]{3,2,1,0:T(2,128)}), f32[32,27,2,128]{3,2,1,0:T(2,128)S(1)}, u32[]{:S(2)}, u32[]{:S(2)}) %all-to-all-start.3) | async-done | bytes 884768 | tf_op jit(solution)/shard_map/all_to_all | solution.py:320
  188.4 3.9 %shard_map.45 = f32[6,192,192]{2,1,0:T(8,128)} custom-call(f32[3]{0:T(128)S(1)} %gather_fusion, f32[1728,128]{1,0:T(8,128)S(1)} %bitcast.16, f32[6,288,128]{2,1,0:T(8,128)S(1)} %shard_map.37.refs_0_.refs_1_.own_ref, f32[6,288,128]{2,1,0:T(8,128)} %copy-done.6, bf16[2560,256]{1,0:T(8,128)(2,1)S(1)} %copy-done), custom_call_target="tpu_custom_call" | custom-call | flops 509607936 | bytes 4194304 | tf_op jit(solution)/shard_map/pallas_call | solution.py:293
  (18 shorter events, 0.1 us)
Async XLA Ops:
  0.0 5.9 %copy-start = (bf16[2560,256]{1,0:T(8,128)(2,1)S(1)}, bf16[2560,256]{1,0:T(8,128)(2,1)}, u32[]{:S(2)}) copy-start(bf16[2560,256]{1,0:T(8,128)(2,1)} %constant.104.clone.refs_3_.refs_2_.table_ref) | copy-start | bytes 3932164
  0.0 1.4 copy-start.3
  1.5 22.7 %collective-permute-start = (f32[6,288,128]{2,1,0:T(8,128)S(1)}, f32[6,288,128]{2,1,0:T(8,128)S(1)}, u32[]{:S(2)}, u32[]{:S(2)}) collective-permute-start(f32[6,288,128]{2,1,0:T(8,128)S(1)} %shard_map.37.refs_0_.refs_1_.own_ref), channel_id=1, source_target_pairs={{0,224},{32,0},{64,32},{96,64},{128,96},{160,128},{192,160},{224,1... | collective-permute-start | bytes 2654216 | tf_op jit(solution)/shard_map/ppermute | solution.py:331
  5.9 21.5 %collective-permute-start.1 = (f32[6,288,128]{2,1,0:T(8,128)S(1)}, f32[6,288,128]{2,1,0:T(8,128)}, u32[]{:S(2)}, u32[]{:S(2)}) collective-permute-start(f32[6,288,128]{2,1,0:T(8,128)S(1)} %shard_map.37.refs_0_.refs_1_.own_ref), channel_id=1, source_target_pairs={{0,64},{32,96},{64,128},{96,160},{128,192},{160,224},{192,0},{224,... | collective-permute-start | bytes 2654216 | tf_op jit(solution)/shard_map/ppermute | solution.py:331
  8.4 36.7 %all-to-all-start = ((f32[32,27,2,128]{3,2,1,0:T(2,128)}), f32[32,27,2,128]{3,2,1,0:T(2,128)}, u32[]{:S(2)}, u32[]{:S(2)}) async-start(f32[32,27,2,128]{3,2,1,0:T(2,128)} %bitcast.5), calls=%async_computation | async-start | bytes 1769472 | tf_op jit(solution)/shard_map/all_to_all | solution.py:320
  24.2 6.9 %copy-start.4 = (f32[6,288,128]{2,1,0:T(8,128)}, f32[6,288,128]{2,1,0:T(8,128)S(1)}, u32[]{:S(2)}) copy-start(f32[6,288,128]{2,1,0:T(8,128)S(1)} %collective-permute-done.refs_1_.refs_0_) | copy-start | bytes 2654212
  31.1 1.2 copy-start.2
  45.1 49.1 %all-to-all-start.1 = ((f32[32,27,4,128]{3,2,1,0:T(4,128)}), f32[32,27,4,128]{3,2,1,0:T(4,128)}, u32[]{:S(2)}, u32[]{:S(2)}) async-start(f32[32,27,4,128]{3,2,1,0:T(4,128)} %bitcast.17), calls=%async_computation.1 | async-start | bytes 3538944 | tf_op jit(solution)/shard_map/all_to_all | solution.py:320
  98.1 1.2 copy-start.1
  99.4 6.3 %copy-start.7 = (s32[8]{0:T(128)S(1)}, s32[8]{0:T(128)}, u32[]{:S(2)}) copy-start(s32[8]{0:T(128)} %param.4) | copy-start | bytes 100
  99.4 49.6 %all-to-all-start.2 = ((f32[32,27,4,128]{3,2,1,0:T(4,128)}), f32[32,27,4,128]{3,2,1,0:T(4,128)}, u32[]{:S(2)}, u32[]{:S(2)}) async-start(f32[32,27,4,128]{3,2,1,0:T(4,128)} %bitcast.15), calls=%async_computation.2 | async-start | bytes 3538944 | tf_op jit(solution)/shard_map/all_to_all | solution.py:320
  153.6 30.3 %collective-permute-start.2 = (f32[6,288,128]{2,1,0:T(8,128)}, f32[6,288,128]{2,1,0:T(8,128)}, u32[]{:S(2)}, u32[]{:S(2)}) collective-permute-start(f32[6,288,128]{2,1,0:T(8,128)} %get-tuple-element.19), channel_id=1, source_target_pairs={{0,32},{32,64},{64,96},{96,128},{128,160},{160,192},{192,224},{224... | collective-permute-start | bytes 2654216 | tf_op jit(solution)/shard_map/ppermute | solution.py:331
  153.6 30.3 %collective-permute-start.3 = (f32[6,288,128]{2,1,0:T(8,128)}, f32[6,288,128]{2,1,0:T(8,128)}, u32[]{:S(2)}, u32[]{:S(2)}) collective-permute-start(f32[6,288,128]{2,1,0:T(8,128)} %get-tuple-element.20), channel_id=1, source_target_pairs={{0,192},{32,224},{64,0},{96,32},{128,64},{160,96},{192,128},{224,1... | collective-permute-start | bytes 2654216 | tf_op jit(solution)/shard_map/ppermute | solution.py:331
  157.3 31.1 %all-to-all-start.3 = ((f32[32,27,2,128]{3,2,1,0:T(2,128)}), f32[32,27,2,128]{3,2,1,0:T(2,128)S(1)}, u32[]{:S(2)}, u32[]{:S(2)}) async-start(f32[32,27,2,128]{3,2,1,0:T(2,128)} %bitcast.11), calls=%async_computation.3 | async-start | bytes 1769472 | tf_op jit(solution)/shard_map/all_to_all | solution.py:320
  163.7 1.2 copy-start.5
  185.5 0.9 copy-start.6

commit v5 on v4

--- a/solution.py
+++ b/solution.py
@@ -231,18 +231,16 @@
     return planes
 
 
-def sent_back(blocks, count, own, weights, table):
+def sent_back(blocks, number, own, weights, table):
     places, entries, rows, length = table
     block = rows * rows * length // LANES
 
-    def kernel(weight, block_ref, own_ref, table_ref, *sent):
-        for number in range(count):
-            made = fields(block_ref, number * block, rows, length // rows, table_ref, places)
-            for plane, field in enumerate(made):
-                sent[number][plane] = (weight[0] * own_ref[plane]) * field
-
-    shape = packed_shape(rows, length)
-    work = call(kernel, [shape] * count, count * 12 * length**3 * rows, count * 2**22, [SMEM] + [VMEM] * 3)
+    def kernel(weight, block_ref, own_ref, table_ref, sent):
+        made = fields(block_ref, number * block, rows, length // rows, table_ref, places)
+        for plane, field in enumerate(made):
+            sent[plane] = (weight[0] * own_ref[plane]) * field
+
+    work = call(kernel, packed_shape(rows, length), 12 * length**3 * rows, 2**22, [SMEM] + [VMEM] * 3)
     return work(weights, blocks, own, entries)
 
 
@@ -267,12 +265,12 @@
 def add_received(partial, received):
     rows = partial.shape[0]
 
-    def kernel(part, first, second, out):
+    def kernel(part, arrived, out):
         for plane in range(rows):
-            out[plane] = part[plane] + (first[plane] + second[plane])
+            out[plane] = part[plane] + arrived[plane]
 
     shape = jax.ShapeDtypeStruct(partial.shape, jnp.float32)
-    return call(kernel, shape, 2**34, 2**22, [VMEM] * 3)(partial, *received)
+    return call(kernel, shape, 2**34, 2**22, [VMEM] * 2)(partial, received)
 
 
 def apply_own(blocks, own, others, weights, table):
@@ -345,10 +343,11 @@
     pair_back = exchange(middle(pair_lines, [0, 1], kernel_values, table))
     own_image, pair_back = lax.optimization_barrier((own_image, pair_back))
     own_back = exchange(own_image)
-    to_next, to_far = sent_back(pair_back, len(guests), own, weights, table)
+    to_next = sent_back(pair_back, 0, own, weights, table)
+    to_far = sent_back(pair_back, 1, own, weights, table)
     partial = guest_terms(pair_back, guests, weights, table)
-    received = [shifted(to_next, 1), shifted(to_far, -2)]
-    others = add_received(partial, received)
+    from_before, from_far = shifted(to_next, 1), shifted(to_far, -2)
+    others = add_received(add_received(partial, from_before), from_far)
     return apply_own(own_back, own, others, weights, table)[None]
 
 

time: 193 us -> 191 us (0.990)
  waiting for transfers between devices: 118 us -> 116 us
    pallas_call x1 -> x2, Pallas kernels: 4.68 us -> 6.68 us  [sent_back(): return work(weights, blocks, own, entries)]
  transfers between devices with their start and end apart: 8 -> 8, of which waited for: 7 -> 6; matrix products, arithmetic and copies ran while one was open for 1% -> 1% of each run, Pallas kernels for 8% -> 10%
where the time goes in v5:
time: 191 us; the launch traced here: 190 us
  waiting for transfers between devices  116 us (61%)
  starting transfers between devices  38.3 us (20%)
  Pallas kernels  30 us (16%)
  local copies, waits for them, and re-layouts  5.38 us (3%)
    all_to_all x4, waiting for transfers between devices, exchange(): lax.all_to_all(cut, 'space', split_axis=0, concat_axis=0, tiled=True)  94.3 us
    all_to_all x4, starting transfers between devices, exchange(): lax.all_to_all(cut, 'space', split_axis=0, concat_axis=0, tiled=True)  30.2 us
    ppermute x4, waiting for transfers between devices, shifted(): lax.ppermute(array, 'band', [(group, (group + by) % groups) for group in...  21.5 us
    ppermute x4, starting transfers between devices, shifted(): lax.ppermute(array, 'band', [(group, (group + by) % groups) for group in...  8.08 us
    pallas_call x2, Pallas kernels, middle(): work(pltpu.with_memory_space_constraint(blocks, pltpu.HBM), kernel_values...  7.78 us
    pallas_call x2, Pallas kernels, sent_back(): return work(weights, blocks, own, entries)  6.68 us
    pallas_call x2, Pallas kernels, forward(): return work(own, *guests, entries)  6.15 us
    unnamed x16, local copies, waits for them, and re-layouts  4.75 us
  transfers between devices with their start and end apart: 8, of which 6 were waited for; matrix products, arithmetic and copies ran while one was open for 1% of the time, Pallas kernels for 10%

profile of v5, /device:TPU:1, one launch (start us, length us, event | category | flops | bytes accessed | tf_op | source)
XLA Modules:
  0.0 190.4 jit_solution(11220892361083685018)
XLA Ops:
  0.0 1.4 copy-done.3
  1.4 0.1 shard_map.37.refs_0_.refs_1_.own_ref
  1.5 4.4 %collective-permute-start = (f32[6,288,128]{2,1,0:T(8,128)S(1)}, f32[6,288,128]{2,1,0:T(8,128)S(1)}, u32[]{:S(2)}, u32[]{:S(2)}) collective-permute-start(f32[6,288,128]{2,1,0:T(8,128)S(1)} %shard_map.37.refs_0_.refs_1_.own_ref), channel_id=1, source_target_pairs={{0,224},{32,0},{64,32},{96,64},{128,96},{160,128},{192,160},{224,1... | collective-permute-start | bytes 2654216 | tf_op jit(solution)/shard_map/ppermute | solution.py:329
  5.9 0.0 collective-permute-start.1
  5.9 2.5 %shard_map.39 = f32[1728,128]{1,0:T(8,128)} custom-call(f32[6,288,128]{2,1,0:T(8,128)S(1)} %shard_map.37.refs_0_.refs_1_.own_ref, f32[6,288,128]{2,1,0:T(8,128)S(1)} %shard_map.37.refs_0_.refs_1_.own_ref, bf16[2560,256]{1,0:T(8,128)(2,1)S(1)} %copy-done), custom_call_target="tpu_custom_call" | custom-call | flops 509607936 | bytes 4194304 | tf_op jit(solution)/shard_map/pallas_call | solution.py:158
  8.4 12.0 %all-to-all-start = ((f32[32,27,2,128]{3,2,1,0:T(2,128)}), f32[32,27,2,128]{3,2,1,0:T(2,128)}, u32[]{:S(2)}, u32[]{:S(2)}) async-start(f32[32,27,2,128]{3,2,1,0:T(2,128)} %bitcast.5), calls=%async_computation | async-start | bytes 1769472 | tf_op jit(solution)/shard_map/all_to_all | solution.py:318
  20.4 3.9 %collective-permute-done.refs_1_.refs_0_ = f32[6,288,128]{2,1,0:T(8,128)S(1)} collective-permute-done((f32[6,288,128]{2,1,0:T(8,128)S(1)}, f32[6,288,128]{2,1,0:T(8,128)S(1)}, u32[]{:S(2)}, u32[]{:S(2)}) %collective-permute-start) | collective-permute-done | bytes 884768 | tf_op jit(solution)/shard_map/ppermute | solution.py:329
  24.2 3.2 %collective-permute-done.1.refs_2_.refs_1_ = f32[6,288,128]{2,1,0:T(8,128)} collective-permute-done((f32[6,288,128]{2,1,0:T(8,128)S(1)}, f32[6,288,128]{2,1,0:T(8,128)}, u32[]{:S(2)}, u32[]{:S(2)}) %collective-permute-start.1) | collective-permute-done | bytes 884768 | tf_op jit(solution)/shard_map/ppermute | solution.py:329
  27.4 3.7 %shard_map.38 = f32[3456,128]{1,0:T(8,128)S(1)} custom-call(f32[6,288,128]{2,1,0:T(8,128)S(1)} %shard_map.37.refs_0_.refs_1_.own_ref, f32[6,288,128]{2,1,0:T(8,128)S(1)} %collective-permute-done.refs_1_.refs_0_, f32[6,288,128]{2,1,0:T(8,128)} %collective-permute-done.1.refs_2_.refs_1_, bf16[2560,256]{1,0:T(8,128)(2,1)S(1)} %copy-done), custom_call_target="tpu_custom_call" | custom-call | flops 16307453952 | bytes 8388608 | tf_op jit(solution)/shard_map/pallas_call | solution.py:158
  31.2 1.2 copy-done.2
  32.4 12.7 %all-to-all-done = f32[32,27,2,128]{3,2,1,0:T(2,128)} async-done(((f32[32,27,2,128]{3,2,1,0:T(2,128)}), f32[32,27,2,128]{3,2,1,0:T(2,128)}, u32[]{:S(2)}, u32[]{:S(2)}) %all-to-all-start) | async-done | bytes 884768 | tf_op jit(solution)/shard_map/all_to_all | solution.py:318
  45.1 5.8 %all-to-all-start.1 = ((f32[32,27,4,128]{3,2,1,0:T(4,128)}), f32[32,27,4,128]{3,2,1,0:T(4,128)}, u32[]{:S(2)}, u32[]{:S(2)}) async-start(f32[32,27,4,128]{3,2,1,0:T(4,128)} %bitcast.17), calls=%async_computation.1 | async-start | bytes 3538944 | tf_op jit(solution)/shard_map/all_to_all | solution.py:318
  50.9 0.3 select_multiply_fusion.values
  51.3 3.8 %shard_map.40 = f32[1728,128]{1,0:T(8,128)} custom-call(f32[1728,128]{1,0:T(8,128)} %bitcast.6.source, f32[192,1152]{1,0:T(8,128)S(1)} %select_multiply_fusion.values, bf16[2560,256]{1,0:T(8,128)(2,1)S(1)} %copy-done), custom_call_target="tpu_custom_call" | custom-call | flops 509607936 | bytes 4718592 | tf_op jit(solution)/shard_map/pallas_call | solution.py:209
  55.1 39.1 %all-to-all-done.1 = f32[32,27,4,128]{3,2,1,0:T(4,128)} async-done(((f32[32,27,4,128]{3,2,1,0:T(4,128)}), f32[32,27,4,128]{3,2,1,0:T(4,128)}, u32[]{:S(2)}, u32[]{:S(2)}) %all-to-all-start.1) | async-done | bytes 1769504 | tf_op jit(solution)/shard_map/all_to_all | solution.py:318
  94.2 3.9 %shard_map.41 = f32[3456,128]{1,0:T(8,128)S(1)} custom-call(f32[3456,128]{1,0:T(8,128)} %bitcast.8.source, f32[192,1152]{1,0:T(8,128)S(1)} %select_multiply_fusion.values, bf16[2560,256]{1,0:T(8,128)(2,1)S(1)} %copy-done), custom_call_target="tpu_custom_call" | custom-call | flops 1019215872 | bytes 9437184 | tf_op jit(solution)/shard_map/pallas_call | solution.py:209
  98.2 1.2 copy-done.1
  99.4 6.3 %all-to-all-start.2 = ((f32[32,27,4,128]{3,2,1,0:T(4,128)}), f32[32,27,4,128]{3,2,1,0:T(4,128)}, u32[]{:S(2)}, u32[]{:S(2)}) async-start(f32[32,27,4,128]{3,2,1,0:T(4,128)} %bitcast.15), calls=%async_computation.2 | async-start | bytes 3538944 | tf_op jit(solution)/shard_map/all_to_all | solution.py:318
  105.7 0.1 fusion.19
  105.8 0.6 gather_fusion
  106.5 42.5 %all-to-all-done.2 = f32[32,27,4,128]{3,2,1,0:T(4,128)} async-done(((f32[32,27,4,128]{3,2,1,0:T(4,128)}), f32[32,27,4,128]{3,2,1,0:T(4,128)}, u32[]{:S(2)}, u32[]{:S(2)}) %all-to-all-start.2) | async-done | bytes 1769504 | tf_op jit(solution)/shard_map/all_to_all | solution.py:318
  149.0 3.8 %shard_map.43 = f32[6,288,128]{2,1,0:T(8,128)} custom-call(f32[3]{0:T(128)S(1)} %gather_fusion, f32[3456,128]{1,0:T(8,128)} %bitcast.10.block_ref, f32[6,288,128]{2,1,0:T(8,128)S(1)} %shard_map.37.refs_0_.refs_1_.own_ref, bf16[2560,256]{1,0:T(8,128)(2,1)S(1)} %copy-done), custom_call_target="tpu_custom_call" | custom-call | flops 509607936 | bytes 4194304 | tf_op jit(solution)/shard_map/pallas_call | solution.py:244
  152.8 0.0 collective-permute-start.2
  152.8 6.2 %all-to-all-start.3 = ((f32[32,27,2,128]{3,2,1,0:T(2,128)}), f32[32,27,2,128]{3,2,1,0:T(2,128)S(1)}, u32[]{:S(2)}, u32[]{:S(2)}) async-start(f32[32,27,2,128]{3,2,1,0:T(2,128)} %bitcast.11), calls=%async_computation.3 | async-start | bytes 1769472 | tf_op jit(solution)/shard_map/all_to_all | solution.py:318
  158.9 2.9 %shard_map.45 = f32[6,288,128]{2,1,0:T(8,128)S(1)} custom-call(f32[3]{0:T(128)S(1)} %gather_fusion, f32[3456,128]{1,0:T(8,128)} %bitcast.10.block_ref, f32[6,288,128]{2,1,0:T(8,128)S(1)} %shard_map.37.refs_0_.refs_1_.own_ref, bf16[2560,256]{1,0:T(8,128)(2,1)S(1)} %copy-done), custom_call_target="tpu_custom_call" | custom-call | flops 509607936 | bytes 4194304 | tf_op jit(solution)/shard_map/pallas_call | solution.py:244
  161.9 3.7 %collective-permute-start.3 = (f32[6,288,128]{2,1,0:T(8,128)S(1)}, f32[6,288,128]{2,1,0:T(8,128)S(1)}, u32[]{:S(2)}, u32[]{:S(2)}) collective-permute-start(f32[6,288,128]{2,1,0:T(8,128)S(1)} %shard_map.45), channel_id=1, source_target_pairs={{0,192},{32,224},{64,0},{96,32},{128,64},{160,96},{192,128},{224,1... | collective-permute-start | bytes 2654216 | tf_op jit(solution)/shard_map/ppermute | solution.py:329
  165.5 4.0 %shard_map.42.part = f32[6,288,128]{2,1,0:T(8,128)S(1)} custom-call(f32[3]{0:T(128)S(1)} %gather_fusion, f32[3456,128]{1,0:T(8,128)} %bitcast.10.block_ref, f32[6,288,128]{2,1,0:T(8,128)S(1)} %copy-done.5, f32[6,288,128]{2,1,0:T(8,128)} %collective-permute-done.1.refs_2_.refs_1_, bf16[2560,256]{1,0:T(8,128)(2,1)S(1)} %copy-done), custom_call_target="tpu_custom_call" | custom-call | flops 1019215872 | bytes 8388608 | tf_op jit(solution)/shard_map/pallas_call | solution.py:262
  169.5 14.5 %collective-permute-done.2.arrived = f32[6,288,128]{2,1,0:T(8,128)} collective-permute-done((f32[6,288,128]{2,1,0:T(8,128)}, f32[6,288,128]{2,1,0:T(8,128)}, u32[]{:S(2)}, u32[]{:S(2)}) %collective-permute-start.2) | collective-permute-done | bytes 884768 | tf_op jit(solution)/shard_map/ppermute | solution.py:329
  184.0 1.3 shard_map.44.part
  185.3 0.1 shard_map.46.other
  185.4 0.9 copy-done.6
  186.3 3.9 %shard_map.47 = f32[6,192,192]{2,1,0:T(8,128)} custom-call(f32[3]{0:T(128)S(1)} %gather_fusion, f32[1728,128]{1,0:T(8,128)S(1)} %bitcast.16, f32[6,288,128]{2,1,0:T(8,128)S(1)} %shard_map.37.refs_0_.refs_1_.own_ref, f32[6,288,128]{2,1,0:T(8,128)} %copy-done.6, bf16[2560,256]{1,0:T(8,128)(2,1)S(1)} %copy-done), custom_call_target="tpu_custom_call" | custom-call | flops 509607936 | bytes 4194304 | tf_op jit(solution)/shard_map/pallas_call | solution.py:291
  (20 shorter events, 0.1 us)
Async XLA Ops:
  0.0 5.9 %copy-start = (bf16[2560,256]{1,0:T(8,128)(2,1)S(1)}, bf16[2560,256]{1,0:T(8,128)(2,1)}, u32[]{:S(2)}) copy-start(bf16[2560,256]{1,0:T(8,128)(2,1)} %constant.104.clone.refs_3_.refs_2_.table_ref) | copy-start | bytes 3932164
  0.0 1.4 copy-start.3
  1.5 22.7 %collective-permute-start = (f32[6,288,128]{2,1,0:T(8,128)S(1)}, f32[6,288,128]{2,1,0:T(8,128)S(1)}, u32[]{:S(2)}, u32[]{:S(2)}) collective-permute-start(f32[6,288,128]{2,1,0:T(8,128)S(1)} %shard_map.37.refs_0_.refs_1_.own_ref), channel_id=1, source_target_pairs={{0,224},{32,0},{64,32},{96,64},{128,96},{160,128},{192,160},{224,1... | collective-permute-start | bytes 2654216 | tf_op jit(solution)/shard_map/ppermute | solution.py:329
  5.9 21.5 %collective-permute-start.1 = (f32[6,288,128]{2,1,0:T(8,128)S(1)}, f32[6,288,128]{2,1,0:T(8,128)}, u32[]{:S(2)}, u32[]{:S(2)}) collective-permute-start(f32[6,288,128]{2,1,0:T(8,128)S(1)} %shard_map.37.refs_0_.refs_1_.own_ref), channel_id=1, source_target_pairs={{0,64},{32,96},{64,128},{96,160},{128,192},{160,224},{192,0},{224,... | collective-permute-start | bytes 2654216 | tf_op jit(solution)/shard_map/ppermute | solution.py:329
  8.4 36.7 %all-to-all-start = ((f32[32,27,2,128]{3,2,1,0:T(2,128)}), f32[32,27,2,128]{3,2,1,0:T(2,128)}, u32[]{:S(2)}, u32[]{:S(2)}) async-start(f32[32,27,2,128]{3,2,1,0:T(2,128)} %bitcast.5), calls=%async_computation | async-start | bytes 1769472 | tf_op jit(solution)/shard_map/all_to_all | solution.py:318
  24.2 6.9 %copy-start.4 = (f32[6,288,128]{2,1,0:T(8,128)}, f32[6,288,128]{2,1,0:T(8,128)S(1)}, u32[]{:S(2)}) copy-start(f32[6,288,128]{2,1,0:T(8,128)S(1)} %collective-permute-done.refs_1_.refs_0_) | copy-start | bytes 2654212
  31.1 1.2 copy-start.2
  45.1 49.1 %all-to-all-start.1 = ((f32[32,27,4,128]{3,2,1,0:T(4,128)}), f32[32,27,4,128]{3,2,1,0:T(4,128)}, u32[]{:S(2)}, u32[]{:S(2)}) async-start(f32[32,27,4,128]{3,2,1,0:T(4,128)} %bitcast.17), calls=%async_computation.1 | async-start | bytes 3538944 | tf_op jit(solution)/shard_map/all_to_all | solution.py:318
  98.1 1.2 copy-start.1
  99.4 6.3 %copy-start.7 = (s32[8]{0:T(128)S(1)}, s32[8]{0:T(128)}, u32[]{:S(2)}) copy-start(s32[8]{0:T(128)} %param.4) | copy-start | bytes 100
  99.4 49.6 %all-to-all-start.2 = ((f32[32,27,4,128]{3,2,1,0:T(4,128)}), f32[32,27,4,128]{3,2,1,0:T(4,128)}, u32[]{:S(2)}, u32[]{:S(2)}) async-start(f32[32,27,4,128]{3,2,1,0:T(4,128)} %bitcast.15), calls=%async_computation.2 | async-start | bytes 3538944 | tf_op jit(solution)/shard_map/all_to_all | solution.py:318
  152.8 31.2 %collective-permute-start.2 = (f32[6,288,128]{2,1,0:T(8,128)}, f32[6,288,128]{2,1,0:T(8,128)}, u32[]{:S(2)}, u32[]{:S(2)}) collective-permute-start(f32[6,288,128]{2,1,0:T(8,128)} %shard_map.43), channel_id=1, source_target_pairs={{0,32},{32,64},{64,96},{96,128},{128,160},{160,192},{192,224},{224... | collective-permute-start | bytes 2654216 | tf_op jit(solution)/shard_map/ppermute | solution.py:329
  152.8 33.6 %all-to-all-start.3 = ((f32[32,27,2,128]{3,2,1,0:T(2,128)}), f32[32,27,2,128]{3,2,1,0:T(2,128)S(1)}, u32[]{:S(2)}, u32[]{:S(2)}) async-start(f32[32,27,2,128]{3,2,1,0:T(2,128)} %bitcast.11), calls=%async_computation.3 | async-start | bytes 1769472 | tf_op jit(solution)/shard_map/all_to_all | solution.py:318
  158.9 6.6 %copy-start.5 = (f32[6,288,128]{2,1,0:T(8,128)S(1)}, f32[6,288,128]{2,1,0:T(8,128)}, u32[]{:S(2)}) copy-start(f32[6,288,128]{2,1,0:T(8,128)} %copy-done.4) | copy-start | bytes 2654212
  161.9 23.4 %collective-permute-start.3 = (f32[6,288,128]{2,1,0:T(8,128)S(1)}, f32[6,288,128]{2,1,0:T(8,128)S(1)}, u32[]{:S(2)}, u32[]{:S(2)}) collective-permute-start(f32[6,288,128]{2,1,0:T(8,128)S(1)} %shard_map.45), channel_id=1, source_target_pairs={{0,192},{32,224},{64,0},{96,32},{128,64},{160,96},{192,128},{224,1... | collective-permute-start | bytes 2654216 | tf_op jit(solution)/shard_map/ppermute | solution.py:329
  185.4 0.9 copy-start.6

commit v6 on v5

--- a/solution.py
+++ b/solution.py
@@ -273,22 +273,26 @@
     return call(kernel, shape, 2**34, 2**22, [VMEM] * 2)(partial, received)
 
 
-def apply_own(blocks, own, others, weights, table):
-    places, entries, rows, length = table
-
-    def kernel(weight, block_ref, own_ref, other, table_ref, out, held, arrived):
+def apply_own(blocks, own, others, last, weights, table):
+    places, entries, rows, length = table
+
+    def kernel(weight, block_ref, own_ref, other, late, table_ref, out, held, late_held, arrived, late_arrived):
         transfer = pltpu.make_async_copy(other, held, arrived)
+        late_transfer = pltpu.make_async_copy(late, late_held, late_arrived)
         transfer.start()
+        late_transfer.start()
         made = fields(block_ref, 0, rows, length // rows, table_ref, places)
         transfer.wait()
+        late_transfer.wait()
         for plane, field in enumerate(made):
-            out[plane] = -unpack(held[plane] + (weight[0] * own_ref[plane]) * field, length)
+            out[plane] = -unpack(held[plane] + late_held[plane] + (weight[0] * own_ref[plane]) * field, length)
 
     shape = jax.ShapeDtypeStruct((rows, length, length), jnp.float32)
-    scratch = [pltpu.VMEM(others.shape, jnp.float32), pltpu.SemaphoreType.DMA(())]
-    work = call(kernel, shape, 12 * length**3 * rows, 2**22, [SMEM, VMEM, VMEM, ANY, VMEM], scratch)
+    scratch = [pltpu.VMEM(others.shape, jnp.float32)] * 2 + [pltpu.SemaphoreType.DMA(())] * 2
+    work = call(kernel, shape, 12 * length**3 * rows, 2**22, [SMEM, VMEM, VMEM, ANY, ANY, VMEM], scratch)
     others = pltpu.with_memory_space_constraint(others, pltpu.HBM)
-    return work(weights, blocks, own, others, entries)
+    last = pltpu.with_memory_space_constraint(last, pltpu.HBM)
+    return work(weights, blocks, own, others, last, entries)
 
 
 def kernel_lines(length, rows, slab):
@@ -347,8 +351,8 @@
     to_far = sent_back(pair_back, 1, own, weights, table)
     partial = guest_terms(pair_back, guests, weights, table)
     from_before, from_far = shifted(to_next, 1), shifted(to_far, -2)
-    others = add_received(add_received(partial, from_before), from_far)
-    return apply_own(own_back, own, others, weights, table)[None]
+    others = add_received(partial, from_before)
+    return apply_own(own_back, own, others, from_far, weights, table)[None]
 
 
 def solution(mesh):

time: 191 us -> 191 us (level)
    unnamed x16 -> x18, local copies, waits for them, and re-layouts: 4.75 us -> 5.64 us
  transfers between devices with their start and end apart: 8 -> 8, of which waited for: 6 -> 6; matrix products, arithmetic and copies ran while one was open for 1% -> 1% of each run, Pallas kernels for 10% -> 9%
where the time goes in v6:
time: 191 us; the launch traced here: 190 us
  waiting for transfers between devices  116 us (61%)
  starting transfers between devices  38.3 us (20%)
  Pallas kernels  29.1 us (15%)
  local copies, waits for them, and re-layouts  6.28 us (3%)
    all_to_all x4, waiting for transfers between devices, exchange(): lax.all_to_all(cut, 'space', split_axis=0, concat_axis=0, tiled=True)  94.3 us
    all_to_all x4, starting transfers between devices, exchange(): lax.all_to_all(cut, 'space', split_axis=0, concat_axis=0, tiled=True)  30.2 us
    ppermute x4, waiting for transfers between devices, shifted(): lax.ppermute(array, 'band', [(group, (group + by) % groups) for group in...  21.5 us
    ppermute x4, starting transfers between devices, shifted(): lax.ppermute(array, 'band', [(group, (group + by) % groups) for group in...  8.08 us
    pallas_call x2, Pallas kernels, middle(): work(pltpu.with_memory_space_constraint(blocks, pltpu.HBM), kernel_values...  6.87 us
    pallas_call x2, Pallas kernels, sent_back(): return work(weights, blocks, own, entries)  6.67 us
    pallas_call x2, Pallas kernels, forward(): return work(own, *guests, entries)  6.15 us
    unnamed x18, local copies, waits for them, and re-layouts  5.64 us
  transfers between devices with their start and end apart: 8, of which 6 were waited for; matrix products, arithmetic and copies ran while one was open for 1% of the time, Pallas kernels for 9%

profile of v6, /device:TPU:1, one launch (start us, length us, event | category | flops | bytes accessed | tf_op | source)
XLA Modules:
  0.0 190.4 jit_solution(5869916317876214073)
XLA Ops:
  0.0 1.4 copy-done.4
  1.4 0.1 shard_map.37.refs_0_.refs_1_.own_ref
  1.5 4.4 %collective-permute-start = (f32[6,288,128]{2,1,0:T(8,128)S(1)}, f32[6,288,128]{2,1,0:T(8,128)S(1)}, u32[]{:S(2)}, u32[]{:S(2)}) collective-permute-start(f32[6,288,128]{2,1,0:T(8,128)S(1)} %shard_map.37.refs_0_.refs_1_.own_ref), channel_id=1, source_target_pairs={{0,224},{32,0},{64,32},{96,64},{128,96},{160,128},{192,160},{224,1... | collective-permute-start | bytes 2654216 | tf_op jit(solution)/shard_map/ppermute | solution.py:333
  5.9 2.5 %shard_map.39 = f32[1728,128]{1,0:T(8,128)} custom-call(f32[6,288,128]{2,1,0:T(8,128)S(1)} %shard_map.37.refs_0_.refs_1_.own_ref, f32[6,288,128]{2,1,0:T(8,128)S(1)} %shard_map.37.refs_0_.refs_1_.own_ref, bf16[2560,256]{1,0:T(8,128)(2,1)S(1)} %copy-done), custom_call_target="tpu_custom_call" | custom-call | flops 509607936 | bytes 4194304 | tf_op jit(solution)/shard_map/pallas_call | solution.py:158
  8.4 12.0 %all-to-all-start = ((f32[32,27,2,128]{3,2,1,0:T(2,128)}), f32[32,27,2,128]{3,2,1,0:T(2,128)}, u32[]{:S(2)}, u32[]{:S(2)}) async-start(f32[32,27,2,128]{3,2,1,0:T(2,128)} %bitcast.5), calls=%async_computation | async-start | bytes 1769472 | tf_op jit(solution)/shard_map/all_to_all | solution.py:322
  20.4 3.9 %collective-permute-done.refs_1_.refs_0_ = f32[6,288,128]{2,1,0:T(8,128)S(1)} collective-permute-done((f32[6,288,128]{2,1,0:T(8,128)S(1)}, f32[6,288,128]{2,1,0:T(8,128)S(1)}, u32[]{:S(2)}, u32[]{:S(2)}) %collective-permute-start) | collective-permute-done | bytes 884768 | tf_op jit(solution)/shard_map/ppermute | solution.py:333
  24.2 3.2 %collective-permute-done.1.refs_2_.refs_1_ = f32[6,288,128]{2,1,0:T(8,128)} collective-permute-done((f32[6,288,128]{2,1,0:T(8,128)S(1)}, f32[6,288,128]{2,1,0:T(8,128)}, u32[]{:S(2)}, u32[]{:S(2)}) %collective-permute-start.1) | collective-permute-done | bytes 884768 | tf_op jit(solution)/shard_map/ppermute | solution.py:333
  27.4 3.7 %shard_map.38 = f32[3456,128]{1,0:T(8,128)S(1)} custom-call(f32[6,288,128]{2,1,0:T(8,128)S(1)} %shard_map.37.refs_0_.refs_1_.own_ref, f32[6,288,128]{2,1,0:T(8,128)S(1)} %collective-permute-done.refs_1_.refs_0_, f32[6,288,128]{2,1,0:T(8,128)} %collective-permute-done.1.refs_2_.refs_1_, bf16[2560,256]{1,0:T(8,128)(2,1)S(1)} %copy-done), custom_call_target="tpu_custom_call" | custom-call | flops 16307453952 | bytes 8388608 | tf_op jit(solution)/shard_map/pallas_call | solution.py:158
  31.2 1.2 copy-done.3
  32.4 12.7 %all-to-all-done = f32[32,27,2,128]{3,2,1,0:T(2,128)} async-done(((f32[32,27,2,128]{3,2,1,0:T(2,128)}), f32[32,27,2,128]{3,2,1,0:T(2,128)}, u32[]{:S(2)}, u32[]{:S(2)}) %all-to-all-start) | async-done | bytes 884768 | tf_op jit(solution)/shard_map/all_to_all | solution.py:322
  45.1 5.8 %all-to-all-start.1 = ((f32[32,27,4,128]{3,2,1,0:T(4,128)}), f32[32,27,4,128]{3,2,1,0:T(4,128)}, u32[]{:S(2)}, u32[]{:S(2)}) async-start(f32[32,27,4,128]{3,2,1,0:T(4,128)} %bitcast.18), calls=%async_computation.1 | async-start | bytes 3538944 | tf_op jit(solution)/shard_map/all_to_all | solution.py:322
  50.9 0.3 select_multiply_fusion.values
  51.3 2.9 %shard_map.40 = f32[1728,128]{1,0:T(8,128)S(1)} custom-call(f32[1728,128]{1,0:T(8,128)} %bitcast.6.source, f32[192,1152]{1,0:T(8,128)S(1)} %select_multiply_fusion.values, bf16[2560,256]{1,0:T(8,128)(2,1)S(1)} %copy-done), custom_call_target="tpu_custom_call" | custom-call | flops 509607936 | bytes 4718592 | tf_op jit(solution)/shard_map/pallas_call | solution.py:209
  54.2 0.0 copy-start.2
  54.2 0.9 copy-done.2
  55.1 39.1 %all-to-all-done.1 = f32[32,27,4,128]{3,2,1,0:T(4,128)} async-done(((f32[32,27,4,128]{3,2,1,0:T(4,128)}), f32[32,27,4,128]{3,2,1,0:T(4,128)}, u32[]{:S(2)}, u32[]{:S(2)}) %all-to-all-start.1) | async-done | bytes 1769504 | tf_op jit(solution)/shard_map/all_to_all | solution.py:322
  94.2 3.9 %shard_map.41 = f32[3456,128]{1,0:T(8,128)S(1)} custom-call(f32[3456,128]{1,0:T(8,128)} %bitcast.8.source, f32[192,1152]{1,0:T(8,128)S(1)} %select_multiply_fusion.values, bf16[2560,256]{1,0:T(8,128)(2,1)S(1)} %copy-done), custom_call_target="tpu_custom_call" | custom-call | flops 1019215872 | bytes 9437184 | tf_op jit(solution)/shard_map/pallas_call | solution.py:209
  98.2 1.2 copy-done.1
  99.4 6.3 %all-to-all-start.2 = ((f32[32,27,4,128]{3,2,1,0:T(4,128)}), f32[32,27,4,128]{3,2,1,0:T(4,128)}, u32[]{:S(2)}, u32[]{:S(2)}) async-start(f32[32,27,4,128]{3,2,1,0:T(4,128)} %bitcast.15), calls=%async_computation.2 | async-start | bytes 3538944 | tf_op jit(solution)/shard_map/all_to_all | solution.py:322
  105.7 0.1 fusion.19
  105.8 0.6 gather_fusion
  106.4 42.5 %all-to-all-done.2 = f32[32,27,4,128]{3,2,1,0:T(4,128)} async-done(((f32[32,27,4,128]{3,2,1,0:T(4,128)}), f32[32,27,4,128]{3,2,1,0:T(4,128)}, u32[]{:S(2)}, u32[]{:S(2)}) %all-to-all-start.2) | async-done | bytes 1769504 | tf_op jit(solution)/shard_map/all_to_all | solution.py:322
  149.0 3.8 %shard_map.43 = f32[6,288,128]{2,1,0:T(8,128)} custom-call(f32[3]{0:T(128)S(1)} %gather_fusion, f32[3456,128]{1,0:T(8,128)} %bitcast.10.block_ref, f32[6,288,128]{2,1,0:T(8,128)S(1)} %shard_map.37.refs_0_.refs_1_.own_ref, bf16[2560,256]{1,0:T(8,128)(2,1)S(1)} %copy-done), custom_call_target="tpu_custom_call" | custom-call | flops 509607936 | bytes 4194304 | tf_op jit(solution)/shard_map/pallas_call | solution.py:244
  152.7 0.0 collective-permute-start.2
  152.7 6.2 %all-to-all-start.3 = ((f32[32,27,2,128]{3,2,1,0:T(2,128)}), f32[32,27,2,128]{3,2,1,0:T(2,128)S(1)}, u32[]{:S(2)}, u32[]{:S(2)}) async-start(f32[32,27,2,128]{3,2,1,0:T(2,128)} %bitcast.17), calls=%async_computation.3 | async-start | bytes 1769472 | tf_op jit(solution)/shard_map/all_to_all | solution.py:322
  158.9 2.9 %shard_map.45 = f32[6,288,128]{2,1,0:T(8,128)S(1)} custom-call(f32[3]{0:T(128)S(1)} %gather_fusion, f32[3456,128]{1,0:T(8,128)} %bitcast.10.block_ref, f32[6,288,128]{2,1,0:T(8,128)S(1)} %shard_map.37.refs_0_.refs_1_.own_ref, bf16[2560,256]{1,0:T(8,128)(2,1)S(1)} %copy-done), custom_call_target="tpu_custom_call" | custom-call | flops 509607936 | bytes 4194304 | tf_op jit(solution)/shard_map/pallas_call | solution.py:244
  161.8 3.7 %collective-permute-start.3 = (f32[6,288,128]{2,1,0:T(8,128)S(1)}, f32[6,288,128]{2,1,0:T(8,128)}, u32[]{:S(2)}, u32[]{:S(2)}) collective-permute-start(f32[6,288,128]{2,1,0:T(8,128)S(1)} %shard_map.45), channel_id=1, source_target_pairs={{0,192},{32,224},{64,0},{96,32},{128,64},{160,96},{192,128},{224,1... | collective-permute-start | bytes 2654216 | tf_op jit(solution)/shard_map/ppermute | solution.py:333
  165.5 4.0 %shard_map.42.part = f32[6,288,128]{2,1,0:T(8,128)S(1)} custom-call(f32[3]{0:T(128)S(1)} %gather_fusion, f32[3456,128]{1,0:T(8,128)} %bitcast.10.block_ref, f32[6,288,128]{2,1,0:T(8,128)S(1)} %copy-done.7, f32[6,288,128]{2,1,0:T(8,128)} %collective-permute-done.1.refs_2_.refs_1_, bf16[2560,256]{1,0:T(8,128)(2,1)S(1)} %copy-done), custom_call_target="tpu_custom_call" | custom-call | flops 1019215872 | bytes 8388608 | tf_op jit(solution)/shard_map/pallas_call | solution.py:262
  169.5 14.5 %collective-permute-done.2.arrived = f32[6,288,128]{2,1,0:T(8,128)} collective-permute-done((f32[6,288,128]{2,1,0:T(8,128)}, f32[6,288,128]{2,1,0:T(8,128)}, u32[]{:S(2)}, u32[]{:S(2)}) %collective-permute-start.2) | collective-permute-done | bytes 884768 | tf_op jit(solution)/shard_map/ppermute | solution.py:333
  184.0 1.3 shard_map.44.other
  185.3 0.9 copy-done.5
  186.2 4.0 %shard_map.46 = f32[6,192,192]{2,1,0:T(8,128)} custom-call(f32[3]{0:T(128)S(1)} %gather_fusion, f32[1728,128]{1,0:T(8,128)S(1)} %bitcast.16, f32[6,288,128]{2,1,0:T(8,128)S(1)} %shard_map.37.refs_0_.refs_1_.own_ref, f32[6,288,128]{2,1,0:T(8,128)} %copy-done.5, f32[6,288,128]{2,1,0:T(8,128)} %collective-permute-done.3.late, bf16[2560,256]{1,0:T(8,128)(2,1)S(1)} %copy-done), custom_call_target="tpu_custom_call" | custom-call | flops 509607936 | bytes 4194304 | tf_op jit(solution)/shard_map/pallas_call | solution.py:295
  (21 shorter events, 0.1 us)
Async XLA Ops:
  0.0 5.9 %copy-start = (bf16[2560,256]{1,0:T(8,128)(2,1)S(1)}, bf16[2560,256]{1,0:T(8,128)(2,1)}, u32[]{:S(2)}) copy-start(bf16[2560,256]{1,0:T(8,128)(2,1)} %constant.104.clone.refs_3_.refs_2_.table_ref) | copy-start | bytes 3932164
  0.0 1.4 copy-start.4
  1.5 22.7 %collective-permute-start = (f32[6,288,128]{2,1,0:T(8,128)S(1)}, f32[6,288,128]{2,1,0:T(8,128)S(1)}, u32[]{:S(2)}, u32[]{:S(2)}) collective-permute-start(f32[6,288,128]{2,1,0:T(8,128)S(1)} %shard_map.37.refs_0_.refs_1_.own_ref), channel_id=1, source_target_pairs={{0,224},{32,0},{64,32},{96,64},{128,96},{160,128},{192,160},{224,1... | collective-permute-start | bytes 2654216 | tf_op jit(solution)/shard_map/ppermute | solution.py:333
  5.9 21.5 %collective-permute-start.1 = (f32[6,288,128]{2,1,0:T(8,128)S(1)}, f32[6,288,128]{2,1,0:T(8,128)}, u32[]{:S(2)}, u32[]{:S(2)}) collective-permute-start(f32[6,288,128]{2,1,0:T(8,128)S(1)} %shard_map.37.refs_0_.refs_1_.own_ref), channel_id=1, source_target_pairs={{0,64},{32,96},{64,128},{96,160},{128,192},{160,224},{192,0},{224,... | collective-permute-start | bytes 2654216 | tf_op jit(solution)/shard_map/ppermute | solution.py:333
  8.4 36.7 %all-to-all-start = ((f32[32,27,2,128]{3,2,1,0:T(2,128)}), f32[32,27,2,128]{3,2,1,0:T(2,128)}, u32[]{:S(2)}, u32[]{:S(2)}) async-start(f32[32,27,2,128]{3,2,1,0:T(2,128)} %bitcast.5), calls=%async_computation | async-start | bytes 1769472 | tf_op jit(solution)/shard_map/all_to_all | solution.py:322
  24.2 6.9 %copy-start.6 = (f32[6,288,128]{2,1,0:T(8,128)}, f32[6,288,128]{2,1,0:T(8,128)S(1)}, u32[]{:S(2)}) copy-start(f32[6,288,128]{2,1,0:T(8,128)S(1)} %collective-permute-done.refs_1_.refs_0_) | copy-start | bytes 2654212
  31.1 1.2 copy-start.3
  45.1 49.1 %all-to-all-start.1 = ((f32[32,27,4,128]{3,2,1,0:T(4,128)}), f32[32,27,4,128]{3,2,1,0:T(4,128)}, u32[]{:S(2)}, u32[]{:S(2)}) async-start(f32[32,27,4,128]{3,2,1,0:T(4,128)} %bitcast.18), calls=%async_computation.1 | async-start | bytes 3538944 | tf_op jit(solution)/shard_map/all_to_all | solution.py:322
  54.2 0.9 copy-start.2
  98.1 1.2 copy-start.1
  99.4 6.3 %copy-start.8 = (s32[8]{0:T(128)S(1)}, s32[8]{0:T(128)}, u32[]{:S(2)}) copy-start(s32[8]{0:T(128)} %param.4) | copy-start | bytes 100
  99.4 49.6 %all-to-all-start.2 = ((f32[32,27,4,128]{3,2,1,0:T(4,128)}), f32[32,27,4,128]{3,2,1,0:T(4,128)}, u32[]{:S(2)}, u32[]{:S(2)}) async-start(f32[32,27,4,128]{3,2,1,0:T(4,128)} %bitcast.15), calls=%async_computation.2 | async-start | bytes 3538944 | tf_op jit(solution)/shard_map/all_to_all | solution.py:322
  152.7 31.2 %collective-permute-start.2 = (f32[6,288,128]{2,1,0:T(8,128)}, f32[6,288,128]{2,1,0:T(8,128)}, u32[]{:S(2)}, u32[]{:S(2)}) collective-permute-start(f32[6,288,128]{2,1,0:T(8,128)} %shard_map.43), channel_id=1, source_target_pairs={{0,32},{32,64},{64,96},{96,128},{128,160},{160,192},{192,224},{224... | collective-permute-start | bytes 2654216 | tf_op jit(solution)/shard_map/ppermute | solution.py:333
  152.7 33.4 %all-to-all-start.3 = ((f32[32,27,2,128]{3,2,1,0:T(2,128)}), f32[32,27,2,128]{3,2,1,0:T(2,128)S(1)}, u32[]{:S(2)}, u32[]{:S(2)}) async-start(f32[32,27,2,128]{3,2,1,0:T(2,128)} %bitcast.17), calls=%async_computation.3 | async-start | bytes 1769472 | tf_op jit(solution)/shard_map/all_to_all | solution.py:322
  158.9 6.6 %copy-start.7 = (f32[6,288,128]{2,1,0:T(8,128)S(1)}, f32[6,288,128]{2,1,0:T(8,128)}, u32[]{:S(2)}) copy-start(f32[6,288,128]{2,1,0:T(8,128)} %copy-done.6) | copy-start | bytes 2654212
  161.8 24.3 %collective-permute-start.3 = (f32[6,288,128]{2,1,0:T(8,128)S(1)}, f32[6,288,128]{2,1,0:T(8,128)}, u32[]{:S(2)}, u32[]{:S(2)}) collective-permute-start(f32[6,288,128]{2,1,0:T(8,128)S(1)} %shard_map.45), channel_id=1, source_target_pairs={{0,192},{32,224},{64,0},{96,32},{128,64},{160,96},{192,128},{224,1... | collective-permute-start | bytes 2654216 | tf_op jit(solution)/shard_map/ppermute | solution.py:333
  185.2 0.9 copy-start.5
